TPU v7x, 32 devices: a whole 2x2x4 slice. The times are simulated.
32 devices in a mesh: ctx: 16 (over z, x, core), tp: 2 (over y).
Axes of the slice: x: 2, y: 2, z: 4, core: 2. Of those that a mesh axis runs over, the one named last changes fastest.
Arguments:
- doc_lengths: int32 [32], replicated, may hold values from 1 to 512, 2048 in all
- ssm_x: bfloat16 [2048, 8192], P('ctx', 'tp'), may hold values from -6 to 6
- ssm_gate: bfloat16 [2048, 8192], P('ctx', 'tp'), may hold values from -6 to 6
- ssm_b: bfloat16 [2048, 2048], P('ctx', 'tp'), may hold values from -6 to 6
- ssm_c: bfloat16 [2048, 2048], P('ctx', 'tp'), may hold values from -0.375 to 0.375
- step_size: float32 [2048, 128], P('ctx', 'tp'), as said below
- decay_rate: float32 [128], P('tp'), as said below
- norm_weight: float32 [8192], P('tp'), may hold values from 0.1 to 1.9
- queries: bfloat16 [2048, 8192], P('ctx', 'tp'), may hold values from -96 to 96
- keys: bfloat16 [2048, 1024], P('ctx', 'tp'), may hold values from -4 to 4
- values: bfloat16 [2048, 1024], P('ctx', 'tp'), may hold values from -6 to 6
Outputs:
- mixed: bfloat16 [2048, 8192], P(('ctx', 'tp'))
- attended: bfloat16 [2048, 8192], P(('ctx', 'tp'))
Inputs may be any that keep to these rules, and one draw needn't show every extreme that they name: `doc_lengths`: every document has at least one token; the longest has exactly 512. `step_size`: Positive. `decay_rate`: Positive, at most 0.04.
All inputs are finite; a program needn't handle non-finite values.
Results may differ from a plain program's by a relative error of at most 0.0049.
Values may be sent and summed in bfloat16 or wider, within the bound.
A program may use at most 192 MiB of HBM per device.

v0:
```python
import functools

import jax
import jax.numpy as jnp
from jax import lax
from jax.experimental import pallas as pl
from jax.experimental.pallas import tpu as pltpu
from jax.sharding import PartitionSpec as P

HEADS = 128
GROUPS = 8
ATT_DIM = 128
DOC_DEVS = 4


NEG_LARGE = -1e30


def for_sending(x):
    return jax.tree.map(lambda a: a.astype(jnp.bfloat16) if a.dtype == jnp.float32 else a, x)


def passed_along(block, axis, distance):
    devices = range(lax.axis_size(axis))
    route = [(i - distance, i) for i in devices if i - distance in devices]
    return lax.ppermute(block, axis, route)


def doc_starts(doc_lengths):
    return jnp.cumsum(doc_lengths) - doc_lengths


def doc_index(positions, starts):
    return jnp.sum((starts[None, :] <= positions[:, None]).astype(jnp.int32), axis=1) - 1


def block_terms(ssm_x, ssm_b, ssm_c, step_size, decay_rate, doc_ids, prev_id, group_heads):
    tok_rows = ssm_x.shape[0]
    head_count = step_size.shape[1]
    group_count = head_count // group_heads
    head_size = ssm_x.shape[1] // head_count
    state_size = ssm_b.shape[1] // group_count
    inputs = ssm_x.reshape(tok_rows, group_count, group_heads, head_size)
    in_proj = ssm_b.reshape(tok_rows, group_count, state_size)
    out_proj = ssm_c.reshape(tok_rows, group_count, state_size)
    log_decay = -(step_size * decay_rate[None, :])
    cumulative = jnp.cumsum(log_decay, axis=0)
    same_doc = doc_ids[:, None] == doc_ids[None, :]
    causal = jnp.arange(tok_rows)[:, None] >= jnp.arange(tok_rows)[None, :]
    allowed = (same_doc & causal)[None]
    spread = cumulative.T[:, :, None] - cumulative.T[:, None, :]
    weights = (
        jnp.where(allowed, jnp.exp(jnp.where(allowed, spread, 0.0)), 0.0) * step_size.T[:, None, :]
    )
    intersection = jnp.einsum("tgn,sgn->gts", out_proj, in_proj, preferred_element_type=jnp.float32)
    mixing = (
        weights.reshape(group_count, group_heads, tok_rows, tok_rows) * intersection[:, None]
    ).astype(jnp.bfloat16)
    y_intra = jnp.einsum("ghts,sghp->tghp", mixing, inputs, preferred_element_type=jnp.float32)
    final_sum = cumulative[-1]
    tail = (
        jnp.exp(final_sum[None, :] - cumulative)
        * step_size
        * (doc_ids == doc_ids[-1]).astype(jnp.float32)[:, None]
    )
    scaled = (
        inputs.astype(jnp.float32) * tail.reshape(tok_rows, group_count, group_heads)[..., None]
    ).astype(jnp.bfloat16)
    state_local = jnp.einsum("sghp,sgn->ghpn", scaled, in_proj, preferred_element_type=jnp.float32)
    entry = jnp.exp(cumulative) * (doc_ids == prev_id).astype(jnp.float32)[:, None]
    transmit = jnp.exp(final_sum) * (doc_ids[-1] == prev_id).astype(jnp.float32)
    return (y_intra, state_local, entry, transmit.reshape(group_count, group_heads))


def finish_rows(y_intra, entry, carried, ssm_c, ssm_gate, norm_weight):
    tok_rows, group_count, group_heads, head_size = y_intra.shape
    out_proj = ssm_c.reshape(tok_rows, group_count, -1).astype(jnp.float32)
    incoming = jnp.einsum("tgn,ghpn->tghp", out_proj, carried, precision=lax.Precision.HIGHEST)
    mixer_out = y_intra + incoming * entry.reshape(tok_rows, group_count, group_heads)[..., None]
    gate_vals = ssm_gate.reshape(tok_rows, group_count, group_heads, head_size).astype(jnp.float32)
    gated = (mixer_out * jax.nn.silu(gate_vals)).reshape(
        tok_rows, group_count, group_heads * head_size
    )
    factor = lax.rsqrt(jnp.mean(gated * gated, axis=2, keepdims=True) + 1e-05)
    return ((gated * factor).reshape(tok_rows, -1) * norm_weight[None, :]).astype(jnp.bfloat16)


def chain_states(earlier, later):
    return (earlier[0] * later[0], later[0][:, :, None, None] * earlier[1] + later[1])


def attention_update(
    carry, query_rows, key_block, value_block, key_pos, query_pos, query_doc, starts
):
    running_max, running_sum, running_acc = carry
    block_rows = key_block.shape[0]
    kv_local = key_block.shape[1] // ATT_DIM
    key_heads = key_block.reshape(block_rows, kv_local, ATT_DIM)
    value_heads = value_block.reshape(block_rows, kv_local, ATT_DIM)
    key_doc = doc_index(key_pos, starts)
    allowed = (query_doc[:, None] == key_doc[None, :]) & (key_pos[None, :] <= query_pos[:, None])
    scores = jnp.einsum(
        "tngd,knd->ngtk", query_rows, key_heads, preferred_element_type=jnp.float32
    ) * ATT_DIM ** (-0.5)
    scores = jnp.where(allowed[None, None], scores, -jnp.inf)
    new_max = jnp.maximum(running_max, jnp.max(scores, axis=3))
    probs = jnp.exp(scores - new_max[..., None])
    factor = jnp.exp(running_max - new_max)
    new_sum = running_sum * factor + jnp.sum(probs, axis=3)
    weighted = jnp.einsum(
        "ngtk,knd->ngtd",
        probs.astype(jnp.bfloat16),
        value_heads,
        preferred_element_type=jnp.float32,
    )
    return (new_max, new_sum, running_acc * factor[..., None] + weighted)


def local_any(
    doc_lengths,
    ssm_x,
    ssm_gate,
    ssm_b,
    ssm_c,
    step_size,
    decay_rate,
    norm_weight,
    queries,
    keys,
    values,
):
    tok_rows = ssm_x.shape[0]
    ctx_index = lax.axis_index("ctx")
    begin = ctx_index * tok_rows
    positions = begin + jnp.arange(tok_rows, dtype=jnp.int32)
    starts = doc_starts(doc_lengths)
    doc_ids = doc_index(positions, starts)
    prev_id = doc_index(jnp.reshape(begin - 1, (1,)), starts)[0]
    group_heads = HEADS // GROUPS
    y_intra, state_local, entry, transmit = block_terms(
        ssm_x, ssm_b, ssm_c, step_size, decay_rate, doc_ids, prev_id, group_heads
    )
    merged = (transmit, state_local)
    for level_bit in range(DOC_DEVS.bit_length() - 1):
        earlier = passed_along(
            (for_sending(merged[0]), for_sending(merged[1])), "ctx", 1 << level_bit
        )
        merged = chain_states(earlier, merged)
    carried = passed_along(merged[1], "ctx", 1)
    mixed_rows = finish_rows(y_intra, entry, carried, ssm_c, ssm_gate, norm_weight)
    kv_local = keys.shape[1] // ATT_DIM
    q_groups = queries.shape[1] // (kv_local * ATT_DIM)
    query_rows = queries.reshape(tok_rows, kv_local, q_groups, ATT_DIM)
    floor_start = jnp.max(jnp.where(starts <= begin, starts, 0))
    query_last = begin + tok_rows - 1
    carry_shape = (kv_local, q_groups, tok_rows)
    initial = (
        jnp.full(carry_shape, NEG_LARGE, jnp.float32),
        jnp.zeros(carry_shape, jnp.float32),
        jnp.zeros(carry_shape + (ATT_DIM,), jnp.float32),
    )

    def visit(carry, key_block, value_block, key_begin):
        block_rows = key_block.shape[0]
        needed = (key_begin <= query_last) & (key_begin + block_rows - 1 >= floor_start)

        def update(inner):
            key_pos = key_begin + jnp.arange(block_rows, dtype=jnp.int32)
            return attention_update(
                inner, query_rows, key_block, value_block, key_pos, positions, doc_ids, starts
            )

        def unchanged(inner):
            return inner

        return lax.cond(needed, update, unchanged, carry)

    totals = visit(initial, keys, values, begin)
    for hop_count in range(1, DOC_DEVS + 1):
        near_keys, near_values = passed_along((keys, values), "ctx", hop_count)
        totals = visit(totals, near_keys, near_values, begin - hop_count * tok_rows)
    final_out = totals[2] / totals[1][..., None]
    attended_rows = (
        jnp.transpose(final_out, (2, 0, 1, 3)).reshape(tok_rows, -1).astype(jnp.bfloat16)
    )
    mixed_local, attended_local = (
        lax.all_to_all(mixed_rows, "tp", split_axis=0, concat_axis=1, tiled=True),
        lax.all_to_all(attended_rows, "tp", split_axis=0, concat_axis=1, tiled=True),
    )
    return (mixed_local, attended_local)


LOG2E = 1.4426950408889634
F32 = jnp.float32
BF16 = jnp.bfloat16
MESH_ID = pl.DeviceIdType.MESH
COLS_LAST = (((1,), (1,)), ((), ()))
ROWS_FIRST = (((0,), (0,)), ((), ()))
PIECES = 4
SHARES = 2
RELAY_AFTER = (0, 2, 3, None)


def dot(a, b, dims=(((1,), (0,)), ((), ())), precision=None):
    return lax.dot_general(a, b, dims, precision=precision, preferred_element_type=F32)


def spread_heads(columns, head, head_size):
    lane = lax.broadcasted_iota(jnp.int32, (columns.shape[0], 128), 1)
    wide = jnp.broadcast_to(columns[:, head : head + 1], lane.shape)
    for k in range(1, 128 // head_size):
        wide = jnp.where(lane >= k * head_size, columns[:, head + k : head + k + 1], wide)
    return wide


def pair_kernel(
    n,
    lengths,
    x_in,
    gate_in,
    b_in,
    c_in,
    step_in,
    q_in,
    k_in,
    v_in,
    rate_ref,
    weight_ref,
    mixed_out,
    attended_out,
    x_s,
    gate_s,
    b_s,
    c_s,
    step_s,
    q_s,
    k_s,
    v_s,
    s_own,
    s_far,
    s_near,
    t_own,
    t_far,
    t_near,
    y_s,
    mixed_s,
    attended_s,
    bias_s,
    l_s,
    lt_s,
    dtt_s,
    tail_s,
    entry_s,
    send_sem,
    recv_sem,
    own_sem,
):
    index = lax.axis_index("ctx")
    tp = lax.axis_index("tp")
    parity, pair = lax.rem(index, 2), lax.div(index, 2)
    odd = lax.rem(pair, 2)
    base = index - parity
    other = 1 - parity
    tok = x_in.shape[0]
    rows = 2 * tok
    width = x_s.shape[1]
    group_heads = HEADS // GROUPS
    heads = step_in.shape[0] // 2
    groups = heads // group_heads
    group_width = width // groups
    state = b_s.shape[1] // groups
    head_size = width // heads
    kv_heads = k_s.shape[1] // ATT_DIM
    q_width = q_s.shape[1] // kv_heads
    piece = group_width // PIECES

    peers = [
        (base + other, tp),
        (index, 1 - tp),
        (base + other, 1 - tp),
        (index + 2 - 4 * odd, tp),
        (lax.rem(index + 4, n), tp),
        (lax.rem(index + n - 4, n), tp),
    ]
    ahead, behind = index + 4 < n, index >= 4
    barrier = pltpu.get_barrier_semaphore()
    for peer in peers:
        pl.semaphore_signal(barrier, inc=1, device_id=peer, device_id_type=MESH_ID)
    pl.semaphore_wait(barrier, len(peers))

    used = [0, 0]

    def slot():
        used[0] += 1
        return used[0] - 1

    def remote(src, dst, peer, k):
        return pltpu.make_async_remote_copy(
            src_ref=src,
            dst_ref=dst,
            send_sem=send_sem.at[k],
            recv_sem=recv_sem.at[k],
            device_id=peer,
            device_id_type=MESH_ID,
        )

    def kept(src, dst):
        used[1] += 1
        copy = pltpu.make_async_copy(src, dst, own_sem.at[used[1] - 1])
        copy.start()
        return copy

    mine = pl.ds(pl.multiple_of(parity * tok, tok), tok)
    sent = []

    def swap(src, dst, cols, skip=0):
        begin, size, total = cols
        give = src.at[:, pl.ds(pl.multiple_of(other * total + begin, 128), size)]
        keep = src.at[:, pl.ds(pl.multiple_of(parity * total + begin, 128), size)]
        at = pl.ds(pl.multiple_of(parity * tok + skip, tok), tok)
        place = dst.at[at, begin : begin + size]
        copy = remote(give, place, peers[0], slot())
        copy.start()
        sent.append(copy)
        own = kept(keep, place)

        def ready():
            own.wait()
            copy.wait_recv()

        return ready

    kv_width = k_s.shape[1]
    ready_k = swap(k_in, k_s, (0, kv_width, kv_width), 2 * rows)
    ready_v = swap(v_in, v_s, (0, kv_width, kv_width), 2 * rows)
    give_rows = pl.ds(pl.multiple_of(other * heads, 8), heads)
    keep_rows = pl.ds(pl.multiple_of(parity * heads, 8), heads)
    copy_step = remote(step_in.at[give_rows], step_s.at[:, mine], peers[0], slot())
    copy_step.start()
    sent.append(copy_step)
    own_step = kept(step_in.at[keep_rows], step_s.at[:, mine])
    ready_b = swap(b_in, b_s, (0, b_s.shape[1], b_s.shape[1]))
    ready_x = [swap(x_in, x_s, (g * group_width, group_width, width)) for g in range(groups)]

    first_pairs = pair < 2

    @pl.when(first_pairs)
    def _():
        k_s[:rows, :] = jnp.zeros((rows, kv_width), BF16)
        v_s[:rows, :] = jnp.zeros((rows, kv_width), BF16)
        s_far[...] = jnp.zeros_like(s_far)
        t_far[...] = jnp.zeros_like(t_far)

    def travel(own, far, near):
        far_slot, near_slot = slot(), slot()
        to_far = remote(own, far, (index + 4, tp), far_slot)
        direct = remote(own, near, peers[3], near_slot)
        relayed = remote(far, near, peers[3], near_slot)

        def start():
            @pl.when(ahead)
            def _():
                to_far.start()

            @pl.when(odd == 0)
            def _():
                direct.start()

        def relay():
            @pl.when(behind & (odd == 1))
            def _():
                to_far.wait_recv()

            @pl.when(odd == 1)
            def _():
                relayed.start()

        def arrive():
            @pl.when(behind & (odd == 0))
            def _():
                to_far.wait_recv()

            direct.wait_recv()

        def close():
            @pl.when(ahead)
            def _():
                to_far.wait_send()

            direct.wait_send()

        return start, relay, arrive, close

    own_rows = pl.ds(2 * rows, rows)
    k_trip = travel(k_s.at[own_rows], k_s.at[pl.ds(0, rows)], k_s.at[pl.ds(rows, rows)])
    v_trip = travel(v_s.at[own_rows], v_s.at[pl.ds(0, rows)], v_s.at[pl.ds(rows, rows)])
    t_trip = travel(t_own, t_far, t_near)
    trips = []
    for k in range(groups * PIECES):
        trips.append(travel(s_own.at[k], s_far.at[k], s_near.at[k]))

    ready_k()
    k_trip[0]()
    ready_v()
    v_trip[0]()

    begin = pair * rows
    row_at = begin - 2 * rows + lax.broadcasted_iota(jnp.int32, (1, 3 * rows), 1)
    col_at = begin + lax.broadcasted_iota(jnp.int32, (rows, 1), 0)
    row_doc = jnp.zeros_like(row_at) - 1
    col_doc = jnp.zeros_like(col_at) - 1
    begun, prev_id, last_id = jnp.int32(0), jnp.int32(-1), jnp.int32(-1)
    for j in range(lengths.shape[0]):
        row_doc += (row_at >= begun).astype(jnp.int32)
        col_doc += (col_at >= begun).astype(jnp.int32)
        prev_id += (begin - 1 >= begun).astype(jnp.int32)
        last_id += (begin + rows - 1 >= begun).astype(jnp.int32)
        begun = begun + lengths[j]
    bias_s[...] = jnp.where((row_doc == col_doc) & (row_at <= col_at), 0.0, NEG_LARGE)

    own_step.wait()
    copy_step.wait_recv()
    low = parity == 0
    pad = jnp.zeros((1, 128 - heads), F32)
    step_t = jnp.concatenate([step_s[...], jnp.zeros((128 - heads, rows), F32)], axis=0)
    step = step_t.T
    rate = jnp.where(low, rate_ref[:, :heads], rate_ref[:, heads:])
    rate = jnp.concatenate([rate, pad], axis=1)
    at = lax.broadcasted_iota(jnp.int32, (rows, rows), 0)
    to = lax.broadcasted_iota(jnp.int32, (rows, rows), 1)
    lower = (to <= at).astype(F32)
    total_decay = dot(lower, -(step * rate), precision=lax.Precision.HIGHEST)
    final_sum = total_decay[rows - 1 :, :]
    l_s[...] = total_decay
    lt_s[...] = total_decay.T
    dtt_s[...] = step_t
    tail_s[...] = jnp.where(col_doc == last_id, jnp.exp(final_sum - total_decay) * step, 0.0)
    entry_s[...] = jnp.where(col_doc == prev_id, jnp.exp(total_decay), 0.0)
    passing = (last_id == prev_id).astype(F32)
    t_own[...] = jnp.broadcast_to(jnp.exp(final_sum) * passing, t_own.shape)
    t_trip[0]()

    per = 128 // head_size
    ready_b()
    for g in range(groups):
        ready_x[g]()
        if g == groups - 1:
            ready_c = swap(c_in, c_s, (0, c_s.shape[1], c_s.shape[1]))
            ready_q = swap(q_in, q_s, (0, q_s.shape[1], q_s.shape[1]))
            ready_gate = swap(gate_in, gate_s, (0, width, width))
        b_t = b_s[:, g * state : (g + 1) * state].T
        for p in range(PIECES):
            parts = []
            for tile in range(piece // 128):
                lead = g * group_width + p * piece + tile * 128
                wide = spread_heads(tail_s[...], lead // head_size, head_size)
                parts.append((x_s[:, lead : lead + 128].astype(F32) * wide).astype(BF16))
            s_own[g * PIECES + p] = dot(b_t, jnp.concatenate(parts, axis=1)).astype(BF16)
            trips[g * PIECES + p][0]()
        (k_trip, v_trip)[g][1]()

    lane = lax.broadcasted_iota(jnp.int32, (rows, 128), 1)
    ready_c()
    for g in range(groups):
        proj = slice(g * state, (g + 1) * state)
        inter = dot(c_s[:, proj], b_s[:, proj], COLS_LAST)
        for tile in range(group_width // 128):
            lead = g * group_width + tile * 128
            for k in range(per):
                h = lead // head_size + k
                spread = l_s[:, h : h + 1] - lt_s[h : h + 1, :]
                w = jnp.exp(spread + bias_s[:, 2 * rows :]) * dtt_s[h : h + 1, :]
                part = dot((w * inter).astype(BF16), x_s[:, lead : lead + 128])
                whole = part if k == 0 else jnp.where(lane >= k * head_size, part, whole)
            y_s[:, lead : lead + 128] = whole
    part_rows = rows // 4
    leaving = []

    def exchange(src, out, g, size, count):
        home = pl.ds(pl.multiple_of((tp * 2 + parity) * count * size + g * size, 128), size)
        cols = slice(g * size, (g + 1) * size)
        for peer, fc, ft in ((peers[1], 0, 1), (peers[2], 1, 1), (peers[0], 1, 0)):
            rank = (other if fc else parity) * 2 + (1 - tp if ft else tp)
            at_rows = pl.ds(pl.multiple_of(rank * part_rows, part_rows), part_rows)
            copy = remote(src.at[at_rows, cols], out.at[:, home], peer, slot())
            copy.start()
            leaving.append(copy)
        at_rows = pl.ds(pl.multiple_of((parity * 2 + tp) * part_rows, part_rows), part_rows)
        leaving.append(kept(src.at[at_rows, cols], out.at[:, home]))

    scale = LOG2E * ATT_DIM ** (-0.5)
    ready_q()
    k_trip[2]()
    v_trip[2]()
    for kv_head in range(kv_heads):
        kv_cols = slice(kv_head * ATT_DIM, (kv_head + 1) * ATT_DIM)

        def one_head(h, carry):
            cols = pl.ds(pl.multiple_of(kv_head * q_width + h * ATT_DIM, ATT_DIM), ATT_DIM)
            scores = dot(q_s[:, cols], k_s[:, kv_cols], COLS_LAST) + bias_s[...]
            top = jnp.max(scores, axis=1, keepdims=True)
            probs = jnp.exp2((scores - top) * scale)
            total = jnp.sum(probs, axis=1, keepdims=True)
            summed = dot(probs.astype(BF16), v_s[:, kv_cols])
            attended_s[:, cols] = (summed / total).astype(BF16)
            return carry

        span = q_width // ATT_DIM // SHARES
        for share in range(SHARES):
            lax.fori_loop(share * span, (share + 1) * span, one_head, 0, unroll=2)
            exchange(attended_s, attended_out, kv_head * SHARES + share, q_width // SHARES, kv_heads * SHARES)
            done = kv_head * SHARES + share
            if done == 0:
                t_trip[1]()
            for k in range(len(trips)):
                if RELAY_AFTER[k * 4 // len(trips)] == done:
                    trips[k][1]()

    ready_gate()
    t_trip[2]()
    for g in range(groups):
        proj = slice(g * state, (g + 1) * state)
        square = jnp.zeros((rows, 128), F32)
        for p in range(PIECES):
            k = g * PIECES + p
            if RELAY_AFTER[k * 4 // len(trips)] is None:
                trips[k][1]()
            trips[k][2]()
            lead = g * group_width + p * piece
            decay = jnp.concatenate(
                [
                    spread_heads(t_near[...], (lead + tile * 128) // head_size, head_size)[:1]
                    for tile in range(piece // 128)
                ],
                axis=1,
            )
            carried = (s_near[k].astype(F32) + decay * s_far[k].astype(F32)).astype(BF16)
            incoming = dot(c_s[:, proj], carried)
            for tile in range(piece // 128):
                cols = slice(lead + tile * 128, lead + tile * 128 + 128)
                wide = spread_heads(entry_s[...], (lead + tile * 128) // head_size, head_size)
                z = gate_s[:, cols].astype(F32)
                total = y_s[:, cols] + incoming[:, tile * 128 : tile * 128 + 128] * wide
                total = total * (z / (1.0 + jnp.exp(-z)))
                y_s[:, cols] = total
                square += total * total
        mean = jnp.sum(square, axis=1, keepdims=True) * (1.0 / group_width)
        factor = lax.rsqrt(mean + 1e-05)
        for tile in range(group_width // 128):
            lead = g * group_width + tile * 128
            cols = slice(lead, lead + 128)
            gain = jnp.where(low, weight_ref[:, cols], weight_ref[:, lead + width : lead + width + 128])
            mixed_s[:, cols] = (y_s[:, cols] * factor * gain).astype(BF16)
        exchange(mixed_s, mixed_out, g, group_width, groups)

    for copy in sent:
        copy.wait_send()
    for trip in [k_trip, v_trip, t_trip] + trips:
        trip[3]()
    for copy in leaving:
        copy.wait()


def local_pair(
    doc_lengths,
    ssm_x,
    ssm_gate,
    ssm_b,
    ssm_c,
    step_size,
    decay_rate,
    norm_weight,
    queries,
    keys,
    values,
):
    tok, width = ssm_x.shape
    rows, half = 2 * tok, width // 2
    groups = step_size.shape[1] * GROUPS // HEADS // 2
    state = ssm_b.shape[1] // (2 * groups)
    piece = half // groups // PIECES
    kv_half = keys.shape[1] // 2
    q_half = queries.shape[1] // 2
    pieces = groups * PIECES
    copies = 16 + 2 * pieces + 6 * SHARES + 6
    any_spec = pl.BlockSpec(memory_space=pl.ANY)
    vmem_spec = pl.BlockSpec(memory_space=pltpu.VMEM)
    part = rows // 4
    scratch = [
        pltpu.VMEM((rows, half), BF16),
        pltpu.VMEM((rows, half), BF16),
        pltpu.VMEM((rows, groups * state), BF16),
        pltpu.VMEM((rows, groups * state), BF16),
        pltpu.VMEM((step_size.shape[1] // 2, rows), F32),
        pltpu.VMEM((rows, q_half), BF16),
        pltpu.VMEM((3 * rows, kv_half), BF16),
        pltpu.VMEM((3 * rows, kv_half), BF16),
        pltpu.VMEM((pieces, state, piece), BF16),
        pltpu.VMEM((pieces, state, piece), BF16),
        pltpu.VMEM((pieces, state, piece), BF16),
        pltpu.VMEM((8, 128), F32),
        pltpu.VMEM((8, 128), F32),
        pltpu.VMEM((8, 128), F32),
        pltpu.VMEM((rows, half), F32),
        pltpu.VMEM((rows, half), BF16),
        pltpu.VMEM((rows, q_half), BF16),
        pltpu.VMEM((rows, 3 * rows), F32),
        pltpu.VMEM((rows, 128), F32),
        pltpu.VMEM((128, rows), F32),
        pltpu.VMEM((128, rows), F32),
        pltpu.VMEM((rows, 128), F32),
        pltpu.VMEM((rows, 128), F32),
        pltpu.SemaphoreType.DMA((copies,)),
        pltpu.SemaphoreType.DMA((copies,)),
        pltpu.SemaphoreType.DMA((copies,)),
    ]
    mixed, attended = pl.pallas_call(
        functools.partial(pair_kernel, lax.axis_size("ctx")),
        out_shape=(
            jax.ShapeDtypeStruct((part, 4 * half), BF16),
            jax.ShapeDtypeStruct((part, 4 * q_half), BF16),
        ),
        in_specs=[pl.BlockSpec(memory_space=pltpu.SMEM)] + [any_spec] * 8 + [vmem_spec] * 2,
        out_specs=(any_spec, any_spec),
        scratch_shapes=scratch,
        compiler_params=pltpu.CompilerParams(collective_id=0, has_side_effects=True),
    )(
        doc_lengths,
        ssm_x,
        ssm_gate,
        ssm_b,
        ssm_c,
        step_size.T,
        queries,
        keys,
        values,
        decay_rate[None, :],
        norm_weight[None, :],
    )
    return (mixed, attended)


def solution(mesh):
    tp = mesh.shape["tp"]
    paired = tp == 2 and mesh.shape["ctx"] % 4 == 0 and mesh.shape["ctx"] > 4 and GROUPS // tp % 2 == 0
    return jax.shard_map(
        local_pair if paired else local_any,
        mesh=mesh,
        in_specs=(
            P(),
            P("ctx", "tp"),
            P("ctx", "tp"),
            P("ctx", "tp"),
            P("ctx", "tp"),
            P("ctx", "tp"),
            P("tp"),
            P("tp"),
            P("ctx", "tp"),
            P("ctx", "tp"),
            P("ctx", "tp"),
        ),
        out_specs=(P(("ctx", "tp"), None), P(("ctx", "tp"), None)),
        check_vma=False,
    )
```

profile of v0, /device:TPU:9, one launch (start us, length us, event | category | flops | bytes accessed | tf_op | source)
XLA Modules:
  0.0 56.0 jit_solution(16639719035167763307)
XLA Ops:
  0.6 52.0 %shard_map.122 = (bf16[64,8192]{1,0:T(8,128)(2,1)}, bf16[64,8192]{1,0:T(8,128)(2,1)}) custom-call(s32[32]{0:T(128)} %lengths.1, bf16[128,4096]{1,0:T(8,128)(2,1)} %x_in.1, bf16[128,4096]{1,0:T(8,128)(2,1)} %gate_in.1, bf16[128,1024]{1,0:T(8,128)(2,1)} %b_in.1, bf16[128,1024]{1,0:T(8,128)(2,1)} %c_in.1, f32[64,128]{1,0:T(8,128)} %bitcast.3, ...), custom_call_target="tpu_custom_call" | custom-call | tf_op jit(solution)/shard_map/pallas_call | solution.py:617
  52.7 0.0 copy-start
  52.7 2.4 %copy.15 = bf16[64,8192]{1,0:T(8,128)(2,1)} copy(bf16[64,8192]{1,0:T(8,128)(2,1)} %get-tuple-element.4) | data formatting | bytes 2097152
  55.0 0.0 copy-done
  55.0 1.0 %copy.16 = bf16[64,8192]{1,0:T(8,128)(2,1)} copy(bf16[64,8192]{1,0:T(8,128)(2,1)S(1)} %copy-done) | data formatting | bytes 2097152
Async XLA Ops:
  52.7 2.4 %copy-start = (bf16[64,8192]{1,0:T(8,128)(2,1)S(1)}, bf16[64,8192]{1,0:T(8,128)(2,1)}, u32[]{:S(2)}) copy-start(bf16[64,8192]{1,0:T(8,128)(2,1)} %get-tuple-element.5) | copy-start | bytes 3145732
where the time goes:
time: 56.3 us; the launch traced here: 56 us
  Pallas kernels  52 us (92%)
  local copies, waits for them, and re-layouts  3.32 us (6%)
  between operations  0.65 us (1%)
    pallas_call x1, Pallas kernels, local_pair(): pl.pallas_call(functools.partial(pair_kernel, lax.axis_size('ctx')), out_...  52 us
    unnamed x4, local copies, waits for them, and re-layouts  3.32 us

commit v1 on v0

v1 whole, which is shorter than its diff:
```python
import functools

import jax
import jax.numpy as jnp
from jax import lax
from jax.experimental import pallas as pl
from jax.experimental.pallas import tpu as pltpu
from jax.sharding import PartitionSpec as P

HEADS = 128
GROUPS = 8
ATT_DIM = 128
DOC_DEVS = 4


NEG_LARGE = -1e30


def for_sending(x):
    return jax.tree.map(lambda a: a.astype(jnp.bfloat16) if a.dtype == jnp.float32 else a, x)


def passed_along(block, axis, distance):
    devices = range(lax.axis_size(axis))
    route = [(i - distance, i) for i in devices if i - distance in devices]
    return lax.ppermute(block, axis, route)


def doc_starts(doc_lengths):
    return jnp.cumsum(doc_lengths) - doc_lengths


def doc_index(positions, starts):
    return jnp.sum((starts[None, :] <= positions[:, None]).astype(jnp.int32), axis=1) - 1


def block_terms(ssm_x, ssm_b, ssm_c, step_size, decay_rate, doc_ids, prev_id, group_heads):
    tok_rows = ssm_x.shape[0]
    head_count = step_size.shape[1]
    group_count = head_count // group_heads
    head_size = ssm_x.shape[1] // head_count
    state_size = ssm_b.shape[1] // group_count
    inputs = ssm_x.reshape(tok_rows, group_count, group_heads, head_size)
    in_proj = ssm_b.reshape(tok_rows, group_count, state_size)
    out_proj = ssm_c.reshape(tok_rows, group_count, state_size)
    log_decay = -(step_size * decay_rate[None, :])
    cumulative = jnp.cumsum(log_decay, axis=0)
    same_doc = doc_ids[:, None] == doc_ids[None, :]
    causal = jnp.arange(tok_rows)[:, None] >= jnp.arange(tok_rows)[None, :]
    allowed = (same_doc & causal)[None]
    spread = cumulative.T[:, :, None] - cumulative.T[:, None, :]
    weights = (
        jnp.where(allowed, jnp.exp(jnp.where(allowed, spread, 0.0)), 0.0) * step_size.T[:, None, :]
    )
    intersection = jnp.einsum("tgn,sgn->gts", out_proj, in_proj, preferred_element_type=jnp.float32)
    mixing = (
        weights.reshape(group_count, group_heads, tok_rows, tok_rows) * intersection[:, None]
    ).astype(jnp.bfloat16)
    y_intra = jnp.einsum("ghts,sghp->tghp", mixing, inputs, preferred_element_type=jnp.float32)
    final_sum = cumulative[-1]
    tail = (
        jnp.exp(final_sum[None, :] - cumulative)
        * step_size
        * (doc_ids == doc_ids[-1]).astype(jnp.float32)[:, None]
    )
    scaled = (
        inputs.astype(jnp.float32) * tail.reshape(tok_rows, group_count, group_heads)[..., None]
    ).astype(jnp.bfloat16)
    state_local = jnp.einsum("sghp,sgn->ghpn", scaled, in_proj, preferred_element_type=jnp.float32)
    entry = jnp.exp(cumulative) * (doc_ids == prev_id).astype(jnp.float32)[:, None]
    transmit = jnp.exp(final_sum) * (doc_ids[-1] == prev_id).astype(jnp.float32)
    return (y_intra, state_local, entry, transmit.reshape(group_count, group_heads))


def finish_rows(y_intra, entry, carried, ssm_c, ssm_gate, norm_weight):
    tok_rows, group_count, group_heads, head_size = y_intra.shape
    out_proj = ssm_c.reshape(tok_rows, group_count, -1).astype(jnp.float32)
    incoming = jnp.einsum("tgn,ghpn->tghp", out_proj, carried, precision=lax.Precision.HIGHEST)
    mixer_out = y_intra + incoming * entry.reshape(tok_rows, group_count, group_heads)[..., None]
    gate_vals = ssm_gate.reshape(tok_rows, group_count, group_heads, head_size).astype(jnp.float32)
    gated = (mixer_out * jax.nn.silu(gate_vals)).reshape(
        tok_rows, group_count, group_heads * head_size
    )
    factor = lax.rsqrt(jnp.mean(gated * gated, axis=2, keepdims=True) + 1e-05)
    return ((gated * factor).reshape(tok_rows, -1) * norm_weight[None, :]).astype(jnp.bfloat16)


def chain_states(earlier, later):
    return (earlier[0] * later[0], later[0][:, :, None, None] * earlier[1] + later[1])


def attention_update(
    carry, query_rows, key_block, value_block, key_pos, query_pos, query_doc, starts
):
    running_max, running_sum, running_acc = carry
    block_rows = key_block.shape[0]
    kv_local = key_block.shape[1] // ATT_DIM
    key_heads = key_block.reshape(block_rows, kv_local, ATT_DIM)
    value_heads = value_block.reshape(block_rows, kv_local, ATT_DIM)
    key_doc = doc_index(key_pos, starts)
    allowed = (query_doc[:, None] == key_doc[None, :]) & (key_pos[None, :] <= query_pos[:, None])
    scores = jnp.einsum(
        "tngd,knd->ngtk", query_rows, key_heads, preferred_element_type=jnp.float32
    ) * ATT_DIM ** (-0.5)
    scores = jnp.where(allowed[None, None], scores, -jnp.inf)
    new_max = jnp.maximum(running_max, jnp.max(scores, axis=3))
    probs = jnp.exp(scores - new_max[..., None])
    factor = jnp.exp(running_max - new_max)
    new_sum = running_sum * factor + jnp.sum(probs, axis=3)
    weighted = jnp.einsum(
        "ngtk,knd->ngtd",
        probs.astype(jnp.bfloat16),
        value_heads,
        preferred_element_type=jnp.float32,
    )
    return (new_max, new_sum, running_acc * factor[..., None] + weighted)


def local_any(
    doc_lengths,
    ssm_x,
    ssm_gate,
    ssm_b,
    ssm_c,
    step_size,
    decay_rate,
    norm_weight,
    queries,
    keys,
    values,
):
    tok_rows = ssm_x.shape[0]
    ctx_index = lax.axis_index("ctx")
    begin = ctx_index * tok_rows
    positions = begin + jnp.arange(tok_rows, dtype=jnp.int32)
    starts = doc_starts(doc_lengths)
    doc_ids = doc_index(positions, starts)
    prev_id = doc_index(jnp.reshape(begin - 1, (1,)), starts)[0]
    group_heads = HEADS // GROUPS
    y_intra, state_local, entry, transmit = block_terms(
        ssm_x, ssm_b, ssm_c, step_size, decay_rate, doc_ids, prev_id, group_heads
    )
    merged = (transmit, state_local)
    for level_bit in range(DOC_DEVS.bit_length() - 1):
        earlier = passed_along(
            (for_sending(merged[0]), for_sending(merged[1])), "ctx", 1 << level_bit
        )
        merged = chain_states(earlier, merged)
    carried = passed_along(merged[1], "ctx", 1)
    mixed_rows = finish_rows(y_intra, entry, carried, ssm_c, ssm_gate, norm_weight)
    kv_local = keys.shape[1] // ATT_DIM
    q_groups = queries.shape[1] // (kv_local * ATT_DIM)
    query_rows = queries.reshape(tok_rows, kv_local, q_groups, ATT_DIM)
    floor_start = jnp.max(jnp.where(starts <= begin, starts, 0))
    query_last = begin + tok_rows - 1
    carry_shape = (kv_local, q_groups, tok_rows)
    initial = (
        jnp.full(carry_shape, NEG_LARGE, jnp.float32),
        jnp.zeros(carry_shape, jnp.float32),
        jnp.zeros(carry_shape + (ATT_DIM,), jnp.float32),
    )

    def visit(carry, key_block, value_block, key_begin):
        block_rows = key_block.shape[0]
        needed = (key_begin <= query_last) & (key_begin + block_rows - 1 >= floor_start)

        def update(inner):
            key_pos = key_begin + jnp.arange(block_rows, dtype=jnp.int32)
            return attention_update(
                inner, query_rows, key_block, value_block, key_pos, positions, doc_ids, starts
            )

        def unchanged(inner):
            return inner

        return lax.cond(needed, update, unchanged, carry)

    totals = visit(initial, keys, values, begin)
    for hop_count in range(1, DOC_DEVS + 1):
        near_keys, near_values = passed_along((keys, values), "ctx", hop_count)
        totals = visit(totals, near_keys, near_values, begin - hop_count * tok_rows)
    final_out = totals[2] / totals[1][..., None]
    attended_rows = (
        jnp.transpose(final_out, (2, 0, 1, 3)).reshape(tok_rows, -1).astype(jnp.bfloat16)
    )
    mixed_local, attended_local = (
        lax.all_to_all(mixed_rows, "tp", split_axis=0, concat_axis=1, tiled=True),
        lax.all_to_all(attended_rows, "tp", split_axis=0, concat_axis=1, tiled=True),
    )
    return (mixed_local, attended_local)


LOG2E = 1.4426950408889634
F32 = jnp.float32
BF16 = jnp.bfloat16
MESH_ID = pl.DeviceIdType.MESH
COLS_LAST = (((1,), (1,)), ((), ()))
ROWS_FIRST = (((0,), (0,)), ((), ()))
PIECE = 128
HEADS_AT_ONCE = 2
MERGE_AFTER = (0, 1, 3, 4, 6, 7)
PASS_AFTER = (5, 6, 7)


def dot(a, b, dims=(((1,), (0,)), ((), ())), precision=None):
    return lax.dot_general(a, b, dims, precision=precision, preferred_element_type=F32)


def spread_heads(columns, head, head_size):
    lane = lax.broadcasted_iota(jnp.int32, (columns.shape[0], 128), 1)
    wide = jnp.broadcast_to(columns[:, head : head + 1], lane.shape)
    for k in range(1, 128 // head_size):
        wide = jnp.where(lane >= k * head_size, columns[:, head + k : head + k + 1], wide)
    return wide


def pair_kernel(
    n,
    lengths,
    x_in,
    gate_in,
    b_in,
    c_in,
    step_in,
    q_in,
    k_in,
    v_in,
    rate_ref,
    weight_ref,
    raw_out,
    sums_out,
    attended_out,
    x_s,
    gate_s,
    b_s,
    c_s,
    step_s,
    q_s,
    kv_s,
    own_s,
    beside_s,
    merged_s,
    behind_s,
    passed_s,
    second_s,
    t_own,
    t_beside,
    coef_s,
    y_s,
    raw_s,
    sums_s,
    attended_s,
    bias_s,
    l_s,
    lt_s,
    dtt_s,
    tail_s,
    entry_s,
    send_sem,
    recv_sem,
    own_sem,
):
    index = lax.axis_index("ctx")
    tp = lax.axis_index("tp")
    parity, pair = lax.rem(index, 2), lax.div(index, 2)
    odd = lax.rem(pair, 2)
    base = index - parity
    other = 1 - parity
    tok = x_in.shape[0]
    rows = 2 * tok
    width = x_s.shape[1]
    group_heads = HEADS // GROUPS
    heads = step_in.shape[0] // 2
    groups = heads // group_heads
    group_width = width // groups
    state = b_s.shape[1] // groups
    head_size = width // heads
    kv_width = kv_s.shape[2]
    kv_heads = kv_width // ATT_DIM
    q_width = q_s.shape[1] // kv_heads
    pieces = group_width // PIECE
    group_of = (odd, 1 - odd)

    core_peer = (base + other, tp)
    tp_peer = (index, 1 - tp)
    cross_peer = (base + other, 1 - tp)
    beside = (index + 2 - 4 * odd, tp)
    barrier = pltpu.get_barrier_semaphore()
    greeted = jnp.int32(3)
    reach = {}
    for step in (2, 4, -2, -4):
        reach[step] = (base + step >= 0) & (base + step < n)
        greeted += 2 * reach[step].astype(jnp.int32)

        @pl.when(reach[step])
        def _():
            for core in range(2):
                peer = (base + step + core, tp)
                pl.semaphore_signal(barrier, inc=1, device_id=peer, device_id_type=MESH_ID)

    for peer in (core_peer, tp_peer, cross_peer):
        pl.semaphore_signal(barrier, inc=1, device_id=peer, device_id_type=MESH_ID)
    pl.semaphore_wait(barrier, greeted)
    ahead, behind = reach[4], reach[-4]

    used = [0, 0, 0]

    def slots(kind, count=1):
        used[kind] += count
        return used[kind] - count

    def remote(src, dst, peer, send, recv):
        return pltpu.make_async_remote_copy(
            src_ref=src,
            dst_ref=dst,
            send_sem=send_sem.at[send],
            recv_sem=recv_sem.at[recv],
            device_id=peer,
            device_id_type=MESH_ID,
        )

    at_mine = pl.multiple_of(parity * tok, tok)
    mine = pl.ds(at_mine, tok)
    closing = []

    def trade(moves, whole):
        send, recv, own = slots(0), slots(1), slots(2)
        for give, keep, place in moves:
            remote(give, place, core_peer, send, recv).start()
            pltpu.make_async_copy(keep, place, own_sem.at[own]).start()
        closing.append(remote(whole, whole, core_peer, send, recv).wait_send)

        def ready():
            pltpu.make_async_copy(whole, whole, own_sem.at[own]).wait()
            remote(whole, whole, core_peer, send, recv).wait_recv()

        return ready

    def by_group(src, dst, local_groups):
        size = dst.shape[1] // groups

        def part(core, local):
            at = core * groups * size + group_of[local] * size
            return src.at[:, pl.ds(pl.multiple_of(at, 128), size)]

        moves, first = [], local_groups[0]
        for local in local_groups:
            place = dst.at[mine, local * size : (local + 1) * size]
            moves.append((part(other, local), part(parity, local), place))
        return trade(moves, dst.at[:tok, first * size : (first + len(local_groups)) * size])

    def part_of(src, core, begin, size, total):
        return src.at[:, pl.ds(pl.multiple_of(core * total + begin, 128), size)]

    @pl.when(pair < 2)
    def _():
        kv_s[:, :rows, :] = jnp.zeros((2, rows, kv_width), BF16)

    @pl.when(pair < 1)
    def _():
        kv_s[:, rows : 2 * rows, :] = jnp.zeros((2, rows, kv_width), BF16)

    past_send = (slots(0), slots(0))
    past_recv = [(slots(1), slots(1)) for head in range(kv_heads)]

    def send_past(head):
        cols = slice(head * ATT_DIM, (head + 1) * ATT_DIM)
        for which, step, skip in ((0, 2, rows), (1, 4, 0)):

            @pl.when(reach[step])
            def _():
                for k, src in enumerate((k_in, v_in)):
                    for core in range(2):
                        remote(
                            part_of(src, core, cols.start, ATT_DIM, kv_width),
                            kv_s.at[k, pl.ds(at_mine + skip, tok), cols],
                            (base + step + core, tp),
                            past_send[which],
                            past_recv[head][which],
                        ).start()

    def wait_past(head):
        cols = slice(head * ATT_DIM, (head + 1) * ATT_DIM)
        for which, step, skip in ((0, -2, rows), (1, -4, 0)):

            @pl.when(reach[step])
            def _():
                place = kv_s.at[:, skip : skip + rows, cols]
                remote(place, place, core_peer, past_send[which], past_recv[head][which]).wait_recv()

    send_past(0)
    moves = []
    for local in range(groups):
        place = step_s.at[local * group_heads : (local + 1) * group_heads, mine]

        def step_part(core):
            at = (core * groups + group_of[local]) * group_heads
            return step_in.at[pl.ds(pl.multiple_of(at, 8), group_heads)]

        moves.append((step_part(other), step_part(parity), place))
    ready_step = trade(moves, step_s.at[:, :tok])
    ready_b = by_group(b_in, b_s, tuple(range(groups)))
    ready_x = {local: by_group(x_in, x_s, (local,)) for local in (1, 0)}
    for head in range(1, kv_heads):
        send_past(head)
    ready_c = by_group(c_in, c_s, tuple(range(groups)))
    moves = []
    for k, src in enumerate((k_in, v_in)):
        give = part_of(src, other, 0, kv_width, kv_width)
        keep = part_of(src, parity, 0, kv_width, kv_width)
        moves.append((give, keep, kv_s.at[k, pl.ds(at_mine + 2 * rows, tok), :]))
    ready_kv = trade(moves, kv_s.at[:, 2 * rows : 2 * rows + tok, :])
    q_all = q_s.shape[1]
    give, keep = part_of(q_in, other, 0, q_all, q_all), part_of(q_in, parity, 0, q_all, q_all)
    ready_q = trade([(give, keep, q_s.at[mine, :])], q_s.at[:tok, :])
    ready_gate = by_group(gate_in, gate_s, tuple(range(groups)))

    @pl.when(pair < 2)
    def _():
        behind_s[...] = jnp.zeros_like(behind_s)

    begin = pair * rows
    row_at = begin - 2 * rows + lax.broadcasted_iota(jnp.int32, (1, 3 * rows), 1)
    col_at = begin + lax.broadcasted_iota(jnp.int32, (rows, 1), 0)
    row_doc = jnp.zeros_like(row_at) - 1
    col_doc = jnp.zeros_like(col_at) - 1
    begun, prev_id, last_id = jnp.int32(0), jnp.int32(-1), jnp.int32(-1)
    for j in range(lengths.shape[0]):
        row_doc += (row_at >= begun).astype(jnp.int32)
        col_doc += (col_at >= begun).astype(jnp.int32)
        prev_id += (begin - 1 >= begun).astype(jnp.int32)
        last_id += (begin + rows - 1 >= begun).astype(jnp.int32)
        begun = begun + lengths[j]
    bias_s[...] = jnp.where((row_doc == col_doc) & (row_at <= col_at), 0.0, NEG_LARGE)

    ready_step()
    step_t = jnp.concatenate([step_s[...], jnp.zeros((128 - heads, rows), F32)], axis=0)
    step = step_t.T
    rates = []
    for local in range(groups):
        rate = jnp.zeros((1, group_heads), F32)
        for k in range(2 * groups):
            here = parity * groups + group_of[local] == k
            rate = jnp.where(here, rate_ref[:, k * group_heads : (k + 1) * group_heads], rate)
        rates.append(rate)
    rate = jnp.concatenate(rates + [jnp.zeros((1, 128 - heads), F32)], axis=1)
    at = lax.broadcasted_iota(jnp.int32, (rows, rows), 0)
    to = lax.broadcasted_iota(jnp.int32, (rows, rows), 1)
    lower = (to <= at).astype(F32)
    total_decay = dot(lower, -(step * rate), precision=lax.Precision.HIGHEST)
    final_sum = total_decay[rows - 1 :, :]
    l_s[...] = total_decay
    lt_s[...] = total_decay.T
    dtt_s[...] = step_t
    tail_s[...] = jnp.where(col_doc == last_id, jnp.exp(final_sum - total_decay) * step, 0.0)
    entry_s[...] = jnp.where(col_doc == prev_id, jnp.exp(total_decay), 0.0)
    passing = (last_id == prev_id).astype(F32)
    t_own[...] = jnp.broadcast_to(jnp.exp(final_sum) * passing, t_own.shape)
    t_trip = remote(t_own, t_beside, beside, slots(0), slots(1))
    t_trip.start()
    closing.append(t_trip.wait_send)

    first_send, first_recv = slots(0), slots(1, pieces)
    merge_send, merge_recv = slots(0), slots(1, pieces)
    pass_send, pass_recv = slots(0), slots(1, pieces)

    def first_trip(k):
        return remote(
            own_s.at[pieces + k], beside_s.at[k], beside, first_send, first_recv + k
        )

    def merge_trip(k):
        return remote(
            merged_s.at[k], behind_s.at[k], (index + 4, tp), merge_send, merge_recv + k
        )

    def pass_trip(k):
        return remote(passed_s.at[k], second_s.at[k], beside, pass_send, pass_recv + k)

    per = 128 // head_size
    ready_b()
    for local in (1, 0):
        ready_x[local]()
        b_t = b_s[:, local * state : (local + 1) * state].T
        for k in range(local * pieces, (local + 1) * pieces, 2):
            parts = []
            for tile in range(2):
                lead = (k + tile) * PIECE
                wide = spread_heads(tail_s[...], lead // head_size, head_size)
                parts.append((x_s[:, lead : lead + PIECE].astype(F32) * wide).astype(BF16))
            made = dot(b_t, jnp.concatenate(parts, axis=1)).astype(BF16)
            for tile in range(2):
                own_s[k + tile] = made[:, tile * PIECE : (tile + 1) * PIECE]
                if local == 1:
                    first_trip(k + tile - pieces).start()

    lane = lax.broadcasted_iota(jnp.int32, (rows, 128), 1)
    ready_c()
    for g in range(groups):
        proj = slice(g * state, (g + 1) * state)
        inter = dot(c_s[:, proj], b_s[:, proj], COLS_LAST)
        for tile in range(group_width // 128):
            lead = g * group_width + tile * 128
            halves = []
            for r in range(0, rows, tok):
                seen = slice(0, r + tok)
                bias = bias_s[r : r + tok, 2 * rows : 2 * rows + r + tok]
                mixing = []
                for h in range(lead // head_size, lead // head_size + per):
                    spread = l_s[r : r + tok, h : h + 1] - lt_s[h : h + 1, seen]
                    w = jnp.exp(spread + bias) * dtt_s[h : h + 1, seen] * inter[r : r + tok, seen]
                    mixing.append(w.astype(BF16))
                both = dot(jnp.concatenate(mixing, axis=0), x_s[seen, lead : lead + 128])
                whole = both[:tok]
                for k in range(1, per):
                    part = both[k * tok : (k + 1) * tok]
                    whole = jnp.where(lane[:tok] >= k * head_size, part, whole)
                y_s[r : r + tok, lead : lead + 128] = whole

    part_rows = rows // 4
    exits = ((tp_peer, 0, 1), (cross_peer, 1, 1), (core_peer, 1, 0))

    def exit_slots():
        return slots(0, 3), slots(1, 3), slots(2)

    def leave(sems, piece_for, home):
        send, recv, own = sems
        for k, (peer, far_core, far_tp) in enumerate(exits):
            src = piece_for(other if far_core else parity, 1 - tp if far_tp else tp)
            remote(src, home, peer, send + k, recv + k).start()
        pltpu.make_async_copy(piece_for(parity, tp), home, own_sem.at[own]).start()

    def settle(sems, whole):
        send, recv, own = sems
        for k, (peer, far_core, far_tp) in enumerate(exits):
            remote(whole, whole, peer, send + k, recv + k).wait()
        pltpu.make_async_copy(whole, whole, own_sem.at[own]).wait()

    def row_part(src, cols):
        def piece_for(core, side):
            at = (core * 2 + side) * part_rows
            return src.at[pl.ds(pl.multiple_of(at, part_rows), part_rows), cols]

        return piece_for

    raw_exit, attended_exit, sums_exit = exit_slots(), exit_slots(), exit_slots()

    def coefficients():
        t_trip.wait_recv()
        even = jnp.broadcast_to(odd == 0, (8, 128))
        row = lax.broadcasted_iota(jnp.int32, (8, 128), 0)
        for k in range(pieces):
            h = k * PIECE // head_size
            ours = spread_heads(t_own[...], h, head_size)
            theirs = spread_heads(t_beside[...], group_heads + h, head_size)
            values = (
                (1.0, ours),
                (theirs, 1.0),
                (1.0, 0.0),
                (ours, 1.0),
                (0.0, 1.0),
                (1.0, theirs),
            )
            table = jnp.zeros((8, 128), F32)
            for j, (if_even, if_odd) in enumerate(values):
                table = jnp.where(row == j, jnp.where(even, if_even, if_odd), table)
            coef_s[:, k * PIECE : (k + 1) * PIECE] = table

    def blend(left, right, k, row):
        cols = slice(k * PIECE, (k + 1) * PIECE)
        total = left[k].astype(F32) * coef_s[row : row + 1, cols]
        total += right[k].astype(F32) * coef_s[row + 1 : row + 2, cols]
        return total.astype(BF16)

    def merge(k):
        first_trip(k).wait_recv()
        merged_s[k] = blend(beside_s, own_s, k, 0)

        @pl.when(ahead)
        def _():
            merge_trip(k).start()

    def pass_on(k):
        @pl.when(behind)
        def _():
            merge_trip(k).wait_recv()

        passed_s[k] = blend(own_s, behind_s, k, 2)
        pass_trip(k).start()

    scale = LOG2E * ATT_DIM ** (-0.5)
    ready_kv()
    ready_q()
    coefficients()
    step_no = 0
    for kv_head in range(kv_heads):
        kv_cols = slice(kv_head * ATT_DIM, (kv_head + 1) * ATT_DIM)
        wait_past(kv_head)
        for lead in range(kv_head * q_width, (kv_head + 1) * q_width, HEADS_AT_ONCE * ATT_DIM):
            for r in range(0, rows, tok):
                seen = slice(r, r + 2 * rows + tok)
                asked = jnp.concatenate(
                    [
                        q_s[r : r + tok, lead + h * ATT_DIM : lead + (h + 1) * ATT_DIM]
                        for h in range(HEADS_AT_ONCE)
                    ],
                    axis=0,
                )
                scores = dot(asked, kv_s[0, seen, kv_cols], COLS_LAST)
                bias = bias_s[r : r + tok, seen]
                scores = scores + jnp.concatenate([bias] * HEADS_AT_ONCE, axis=0)
                top = jnp.max(scores, axis=1, keepdims=True)
                probs = jnp.exp2((scores - top) * scale)
                total = jnp.sum(probs, axis=1, keepdims=True)
                summed = dot(probs.astype(BF16), kv_s[1, seen, kv_cols]) / total
                for h in range(HEADS_AT_ONCE):
                    cols = slice(lead + h * ATT_DIM, lead + (h + 1) * ATT_DIM)
                    attended_s[r : r + tok, cols] = summed[h * tok : (h + 1) * tok].astype(BF16)
            size = HEADS_AT_ONCE * ATT_DIM
            at = pl.multiple_of((tp * 2 + parity) * q_all + lead, 128)
            home = attended_out.at[:, pl.ds(at, size)]
            leave(attended_exit, row_part(attended_s, slice(lead, lead + size)), home)
            for k in range(len(MERGE_AFTER)):
                if MERGE_AFTER[k] == step_no:
                    merge(k)
            for k in range(len(PASS_AFTER)):
                if PASS_AFTER[k] == step_no:
                    pass_on(k)
            step_no += 1

    ones = jnp.ones((8, 128), F32)
    squares = [jnp.zeros((rows, 128), F32)] * groups

    def finish(local, first):
        carried = []
        for k in range(first, first + 2):
            if local == 0:
                carried.append(blend(beside_s, behind_s, k, 4))
            else:
                pass_trip(k).wait_recv()
                carried.append(second_s[k])
        proj = slice(local * state, (local + 1) * state)
        incoming = dot(c_s[:, proj], jnp.concatenate(carried, axis=1))
        lead = local * group_width + first * PIECE
        square = squares[local]
        for tile in range(0, 2 * PIECE, 128):
            cols = slice(lead + tile, lead + tile + 128)
            wide = spread_heads(entry_s[...], cols.start // head_size, head_size)
            z = gate_s[:, cols].astype(F32)
            total = y_s[:, cols] + incoming[:, tile : tile + 128] * wide
            total = total * (z / (1.0 + jnp.exp(-z)))
            square += total * total
            at = parity * width + group_of[local] * group_width + first * PIECE + tile
            gain = weight_ref[:, pl.ds(pl.multiple_of(at, 128), 128)]
            raw_s[:, cols] = (total * gain).astype(BF16)
        squares[local] = square
        at = (tp * 2 + parity) * width + group_of[local] * group_width + first * PIECE
        home = raw_out.at[:, pl.ds(pl.multiple_of(at, 128), 2 * PIECE)]
        leave(raw_exit, row_part(raw_s, slice(lead, lead + 2 * PIECE)), home)
        if first + 2 == pieces:
            here = slice(local * 8, local * 8 + 8)
            sums_s[here, :] = dot(ones, square, COLS_LAST, lax.Precision.HIGHEST)
            at = ((tp * 2 + parity) * groups + group_of[local]) * 8
            home = sums_out.at[pl.ds(pl.multiple_of(at, 8), 8), :]

            def half(core, side):
                return sums_s.at[here, pl.ds(pl.multiple_of(core * tok, tok), tok)]

            leave(sums_exit, half, home)

    ready_gate()
    for k in range(len(MERGE_AFTER), pieces):
        merge(k)
    passed = len(PASS_AFTER)
    for k in range(0, pieces, 2):
        while passed < min(pieces, k + 4):
            pass_on(passed)
            passed += 1
        finish(0, k)
    for k in range(0, pieces, 2):
        finish(1, k)

    assert used == [send_sem.shape[0], recv_sem.shape[0], own_sem.shape[0]], used
    for close in closing:
        close()
    for which, step in ((0, 2), (1, 4)):

        @pl.when(reach[step])
        def _():
            place = kv_s.at[:, :rows, :]
            remote(place, place, core_peer, past_send[which], past_recv[0][which]).wait_send()

    half = own_s.at[:pieces]
    remote(half, half, beside, first_send, first_recv).wait_send()
    remote(half, half, beside, pass_send, pass_recv).wait_send()

    @pl.when(ahead)
    def _():
        remote(half, half, beside, merge_send, merge_recv).wait_send()

    settle(attended_exit, attended_s.at[:part_rows, :])
    settle(raw_exit, raw_s.at[:part_rows, :])
    settle(sums_exit, sums_s.at[:, :tok])


def scale_kernel(raw, sums, attended, mixed_out, attended_out, mixed_s, sem):
    tp = lax.axis_index("tp")
    rows, width = raw.shape
    group_width = width // GROUPS
    whole = pltpu.make_async_copy(attended, attended_out, sem.at[GROUPS])
    whole.start()
    squares = sums[...]
    squares = jnp.concatenate([squares, jnp.zeros((128 - squares.shape[0], 128), F32)], axis=0).T
    squares = jnp.where(tp == 0, squares[:rows], squares[rows:])
    factor = lax.rsqrt(squares * (1.0 / group_width) + 1e-05)
    copies = [whole]
    for g in range(GROUPS):
        cols = slice(g * group_width, (g + 1) * group_width)
        mixed_s[:, cols] = (raw[:, cols].astype(F32) * factor[:, 8 * g : 8 * g + 1]).astype(BF16)
        copy = pltpu.make_async_copy(mixed_s.at[:, cols], mixed_out.at[:, cols], sem.at[g])
        copy.start()
        copies.append(copy)
    for copy in copies:
        copy.wait()


def local_pair(
    doc_lengths,
    ssm_x,
    ssm_gate,
    ssm_b,
    ssm_c,
    step_size,
    decay_rate,
    norm_weight,
    queries,
    keys,
    values,
):
    tok, width = ssm_x.shape
    rows, half = 2 * tok, width // 2
    groups = step_size.shape[1] * GROUPS // HEADS // 2
    state = ssm_b.shape[1] // (2 * groups)
    kv_half = keys.shape[1] // 2
    q_half = queries.shape[1] // 2
    pieces = half // PIECE
    any_spec = pl.BlockSpec(memory_space=pl.ANY)
    vmem_spec = pl.BlockSpec(memory_space=pltpu.VMEM)
    part = rows // 4
    group_pieces = pieces // groups
    state_piece = pltpu.VMEM((group_pieces, state, PIECE), BF16)
    scratch = [
        pltpu.VMEM((rows, half), BF16),
        pltpu.VMEM((rows, half), BF16),
        pltpu.VMEM((rows, groups * state), BF16),
        pltpu.VMEM((rows, groups * state), BF16),
        pltpu.VMEM((step_size.shape[1] // 2, rows), F32),
        pltpu.VMEM((rows, q_half), BF16),
        pltpu.VMEM((2, 3 * rows, kv_half), BF16),
        pltpu.VMEM((pieces, state, PIECE), BF16),
        state_piece,
        state_piece,
        state_piece,
        state_piece,
        state_piece,
        pltpu.VMEM((8, 128), F32),
        pltpu.VMEM((8, 128), F32),
        pltpu.VMEM((8, half // groups), F32),
        pltpu.VMEM((rows, half), F32),
        pltpu.VMEM((rows, half), BF16),
        pltpu.VMEM((8 * groups, rows), F32),
        pltpu.VMEM((rows, q_half), BF16),
        pltpu.VMEM((rows, 3 * rows), F32),
        pltpu.VMEM((rows, 128), F32),
        pltpu.VMEM((128, rows), F32),
        pltpu.VMEM((128, rows), F32),
        pltpu.VMEM((rows, 128), F32),
        pltpu.VMEM((rows, 128), F32),
        pltpu.SemaphoreType.DMA((23,)),
        pltpu.SemaphoreType.DMA((18 + kv_half // ATT_DIM * 2 + 3 * group_pieces,)),
        pltpu.SemaphoreType.DMA((11,)),
    ]
    raw, sums, attended = pl.pallas_call(
        functools.partial(pair_kernel, lax.axis_size("ctx")),
        out_shape=(
            pltpu.VMEM((part, 4 * half), BF16),
            pltpu.VMEM((8 * GROUPS, tok), F32),
            pltpu.VMEM((part, 4 * q_half), BF16),
        ),
        in_specs=[pl.BlockSpec(memory_space=pltpu.SMEM)] + [any_spec] * 8 + [vmem_spec] * 2,
        out_specs=(vmem_spec, vmem_spec, vmem_spec),
        scratch_shapes=scratch,
        compiler_params=pltpu.CompilerParams(collective_id=0, has_side_effects=True),
    )(
        doc_lengths,
        ssm_x,
        ssm_gate,
        ssm_b,
        ssm_c,
        step_size.T,
        queries,
        keys,
        values,
        decay_rate[None, :],
        norm_weight[None, :],
    )
    return pl.pallas_call(
        scale_kernel,
        out_shape=(
            jax.ShapeDtypeStruct(raw.shape, BF16),
            jax.ShapeDtypeStruct(attended.shape, BF16),
        ),
        in_specs=[vmem_spec] * 3,
        out_specs=(any_spec, any_spec),
        scratch_shapes=[pltpu.VMEM(raw.shape, BF16), pltpu.SemaphoreType.DMA((GROUPS + 1,))],
    )(*[pltpu.with_memory_space_constraint(a, pltpu.VMEM) for a in (raw, sums, attended)])


def solution(mesh):
    tp = mesh.shape["tp"]
    paired = tp == 2 and mesh.shape["ctx"] % 4 == 0 and mesh.shape["ctx"] > 4 and GROUPS // tp % 2 == 0
    return jax.shard_map(
        local_pair if paired else local_any,
        mesh=mesh,
        in_specs=(
            P(),
            P("ctx", "tp"),
            P("ctx", "tp"),
            P("ctx", "tp"),
            P("ctx", "tp"),
            P("ctx", "tp"),
            P("tp"),
            P("tp"),
            P("ctx", "tp"),
            P("ctx", "tp"),
            P("ctx", "tp"),
        ),
        out_specs=(P(("ctx", "tp"), None), P(("ctx", "tp"), None)),
        check_vma=False,
    )
```

time: 56.3 us -> 40.9 us (0.73)
  the two profiles are of different devices: /device:TPU:9 before, /device:TPU:25 now
where the time goes in v1:
time: 40.9 us; the launch traced here: 40.5 us
  Pallas kernels  39.7 us (97%)
  between operations  0.8 us (2%)
    pallas_call x1, Pallas kernels, local_pair(): pl.pallas_call(functools.partial(pair_kernel, lax.axis_size('ctx')), out_...  38.4 us
    pallas_call x1, Pallas kernels, local_pair(): pl.pallas_call(scale_kernel, out_shape=(jax.ShapeDtypeStruct(raw.shape, B...  1.38 us

profile of v1, /device:TPU:25, one launch (start us, length us, event | category | flops | bytes accessed | tf_op | source)
XLA Modules:
  0.0 40.5 jit_solution(1316621520490801163)
XLA Ops:
  0.6 38.4 %shard_map.122 = (bf16[64,8192]{1,0:T(8,128)(2,1)S(1)}, f32[64,128]{1,0:T(8,128)S(1)}, bf16[64,8192]{1,0:T(8,128)(2,1)S(1)}) custom-call(s32[32]{0:T(128)} %lengths.1, bf16[128,4096]{1,0:T(8,128)(2,1)} %x_in.1, bf16[128,4096]{1,0:T(8,128)(2,1)} %gate_in.1, bf16[128,1024]{1,0:T(8,128)(2,1)} %b_in.1, bf16[128,1024]{1,0:T(8,128)(2,1)} %c_in.1, ...), custom_call_target="tpu_custom_call" | custom-call | tf_op jit(solution)/shard_map/pallas_call | solution.py:783
  39.0 1.4 %shard_map.123 = (bf16[64,8192]{1,0:T(8,128)(2,1)}, bf16[64,8192]{1,0:T(8,128)(2,1)}) custom-call(bf16[64,8192]{1,0:T(8,128)(2,1)S(1)} %get-tuple-element.5.raw, f32[64,128]{1,0:T(8,128)S(1)} %get-tuple-element.6.sums, bf16[64,8192]{1,0:T(8,128)(2,1)S(1)} %get-tuple-element.7.attended), custom_call_target="tpu_custom_call" | custom-call | tf_op jit(solution)/shard_map/pallas_call | solution.py:807

commit v2 on v1

--- a/solution.py
+++ b/solution.py
@@ -198,8 +198,8 @@
 ROWS_FIRST = (((0,), (0,)), ((), ()))
 PIECE = 128
 HEADS_AT_ONCE = 2
-MERGE_AFTER = (0, 1, 3, 4, 6, 7)
-PASS_AFTER = (5, 6, 7)
+MERGE_AFTER = (1, 2, 3, 5, 6, 7)
+PASS_AFTER = (4, 5, 7)
 
 
 def dot(a, b, dims=(((1,), (0,)), ((), ())), precision=None):
@@ -246,6 +246,7 @@
     t_own,
     t_beside,
     coef_s,
+    loan_s,
     y_s,
     raw_s,
     sums_s,
@@ -300,7 +301,6 @@
 
     for peer in (core_peer, tp_peer, cross_peer):
         pl.semaphore_signal(barrier, inc=1, device_id=peer, device_id_type=MESH_ID)
-    pl.semaphore_wait(barrier, greeted)
     ahead, behind = reach[4], reach[-4]
 
     used = [0, 0, 0]
@@ -326,15 +326,18 @@
     def trade(moves, whole):
         send, recv, own = slots(0), slots(1), slots(2)
         for give, keep, place in moves:
-            remote(give, place, core_peer, send, recv).start()
             pltpu.make_async_copy(keep, place, own_sem.at[own]).start()
         closing.append(remote(whole, whole, core_peer, send, recv).wait_send)
+
+        def start():
+            for give, keep, place in moves:
+                remote(give, place, core_peer, send, recv).start()
 
         def ready():
             pltpu.make_async_copy(whole, whole, own_sem.at[own]).wait()
             remote(whole, whole, core_peer, send, recv).wait_recv()
 
-        return ready
+        return start, ready
 
     def by_group(src, dst, local_groups):
         size = dst.shape[1] // groups
@@ -362,33 +365,62 @@
 
     past_send = (slots(0), slots(0))
     past_recv = [(slots(1), slots(1)) for head in range(kv_heads)]
-
-    def send_past(head):
-        cols = slice(head * ATT_DIM, (head + 1) * ATT_DIM)
-        for which, step, skip in ((0, 2, rows), (1, 4, 0)):
+    loan_send, loan_recv = slots(0), slots(1)
+
+    def head_cols(head):
+        return slice(head * ATT_DIM, (head + 1) * ATT_DIM)
+
+    def send_past(head, dst, step, skip, which, recv):
+        for k, src in enumerate((k_in, v_in)):
+            for core in range(2):
+                remote(
+                    part_of(src, core, head * ATT_DIM, ATT_DIM, kv_width),
+                    dst.at[k, pl.ds(at_mine + skip, tok), :],
+                    (base + step + core, tp),
+                    which,
+                    recv,
+                ).start()
+
+    def send_near(head):
+        near = kv_s.at[:, :, head_cols(head)]
+
+        @pl.when(reach[2] & ((odd == 0) | (head == 0)))
+        def _():
+            send_past(head, near, 2, rows, past_send[0], past_recv[head][0])
+
+    def lend():
+        @pl.when(odd == 1)
+        def _():
+            for head in range(1, kv_heads):
+                send_past(head, loan_s.at[:, :, head_cols(head - 1)], -2, 0, loan_send, loan_recv)
+
+    def send_far(head):
+        @pl.when(reach[4])
+        def _():
+            far = kv_s.at[:, :, head_cols(head)]
+            send_past(head, far, 4, 0, past_send[1], past_recv[head][1])
+
+    def near_loan():
+        return kv_s.at[:, rows : 2 * rows, ATT_DIM:]
+
+    def forward():
+        @pl.when(odd == 0)
+        def _():
+            remote(loan_s, loan_s, core_peer, loan_send, loan_recv).wait_recv()
+
+        @pl.when((odd == 0) & ahead)
+        def _():
+            peer = (index + 4, tp)
+            remote(loan_s, near_loan(), peer, loan_send, past_recv[1][0]).start()
+
+    def wait_past(head):
+        for which, step, skip in ((0, -2, rows), (1, -4, 0)):
 
             @pl.when(reach[step])
             def _():
-                for k, src in enumerate((k_in, v_in)):
-                    for core in range(2):
-                        remote(
-                            part_of(src, core, cols.start, ATT_DIM, kv_width),
-                            kv_s.at[k, pl.ds(at_mine + skip, tok), cols],
-                            (base + step + core, tp),
-                            past_send[which],
-                            past_recv[head][which],
-                        ).start()
-
-    def wait_past(head):
-        cols = slice(head * ATT_DIM, (head + 1) * ATT_DIM)
-        for which, step, skip in ((0, -2, rows), (1, -4, 0)):
-
-            @pl.when(reach[step])
-            def _():
-                place = kv_s.at[:, skip : skip + rows, cols]
+                place = kv_s.at[:, skip : skip + rows, head_cols(head)]
                 remote(place, place, core_peer, past_send[which], past_recv[head][which]).wait_recv()
 
-    send_past(0)
     moves = []
     for local in range(groups):
         place = step_s.at[local * group_heads : (local + 1) * group_heads, mine]
@@ -398,22 +430,20 @@
             return step_in.at[pl.ds(pl.multiple_of(at, 8), group_heads)]
 
         moves.append((step_part(other), step_part(parity), place))
-    ready_step = trade(moves, step_s.at[:, :tok])
-    ready_b = by_group(b_in, b_s, tuple(range(groups)))
-    ready_x = {local: by_group(x_in, x_s, (local,)) for local in (1, 0)}
-    for head in range(1, kv_heads):
-        send_past(head)
-    ready_c = by_group(c_in, c_s, tuple(range(groups)))
+    start_step, ready_step = trade(moves, step_s.at[:, :tok])
+    start_b, ready_b = by_group(b_in, b_s, tuple(range(groups)))
+    trade_x = {local: by_group(x_in, x_s, (local,)) for local in (1, 0)}
+    start_c, ready_c = by_group(c_in, c_s, tuple(range(groups)))
     moves = []
     for k, src in enumerate((k_in, v_in)):
         give = part_of(src, other, 0, kv_width, kv_width)
         keep = part_of(src, parity, 0, kv_width, kv_width)
         moves.append((give, keep, kv_s.at[k, pl.ds(at_mine + 2 * rows, tok), :]))
-    ready_kv = trade(moves, kv_s.at[:, 2 * rows : 2 * rows + tok, :])
+    start_kv, ready_kv = trade(moves, kv_s.at[:, 2 * rows : 2 * rows + tok, :])
     q_all = q_s.shape[1]
     give, keep = part_of(q_in, other, 0, q_all, q_all), part_of(q_in, parity, 0, q_all, q_all)
-    ready_q = trade([(give, keep, q_s.at[mine, :])], q_s.at[:tok, :])
-    ready_gate = by_group(gate_in, gate_s, tuple(range(groups)))
+    start_q, ready_q = trade([(give, keep, q_s.at[mine, :])], q_s.at[:tok, :])
+    start_gate, ready_gate = by_group(gate_in, gate_s, tuple(range(groups)))
 
     @pl.when(pair < 2)
     def _():
@@ -433,6 +463,19 @@
         begun = begun + lengths[j]
     bias_s[...] = jnp.where((row_doc == col_doc) & (row_at <= col_at), 0.0, NEG_LARGE)
 
+    pl.semaphore_wait(barrier, greeted)
+    send_near(0)
+    start_step()
+    start_b()
+    send_far(0)
+    for local in (1, 0):
+        trade_x[local][0]()
+    for head in range(1, kv_heads):
+        send_near(head)
+        send_far(head)
+    for start in (start_c, start_kv, start_q, start_gate):
+        start()
+
     ready_step()
     step_t = jnp.concatenate([step_s[...], jnp.zeros((128 - heads, rows), F32)], axis=0)
     step = step_t.T
@@ -446,8 +489,16 @@
     rate = jnp.concatenate(rates + [jnp.zeros((1, 128 - heads), F32)], axis=1)
     at = lax.broadcasted_iota(jnp.int32, (rows, rows), 0)
     to = lax.broadcasted_iota(jnp.int32, (rows, rows), 1)
-    lower = (to <= at).astype(F32)
-    total_decay = dot(lower, -(step * rate), precision=lax.Precision.HIGHEST)
+    lower = (to <= at).astype(BF16)
+    left, parts = -(step * rate), []
+    for k in range(3):
+        parts.append(left.astype(BF16)[:, :heads])
+        left = left - left.astype(BF16).astype(F32)
+    parts.append(jnp.zeros((rows, 128 - 3 * heads), BF16))
+    sums = dot(lower, jnp.concatenate(parts, axis=1))
+    lane = lax.broadcasted_iota(jnp.int32, (rows, 128), 1)
+    sums = sums + pltpu.roll(sums, 128 - heads, 1) + pltpu.roll(sums, 128 - 2 * heads, 1)
+    total_decay = jnp.where(lane < heads, sums, 0.0)
     final_sum = total_decay[rows - 1 :, :]
     l_s[...] = total_decay
     lt_s[...] = total_decay.T
@@ -478,9 +529,10 @@
         return remote(passed_s.at[k], second_s.at[k], beside, pass_send, pass_recv + k)
 
     per = 128 // head_size
+    lend()
     ready_b()
     for local in (1, 0):
-        ready_x[local]()
+        trade_x[local][1]()
         b_t = b_s[:, local * state : (local + 1) * state].T
         for k in range(local * pieces, (local + 1) * pieces, 2):
             parts = []
@@ -494,7 +546,6 @@
                 if local == 1:
                     first_trip(k + tile - pieces).start()
 
-    lane = lax.broadcasted_iota(jnp.int32, (rows, 128), 1)
     ready_c()
     for g in range(groups):
         proj = slice(g * state, (g + 1) * state)
@@ -536,13 +587,6 @@
             remote(whole, whole, peer, send + k, recv + k).wait()
         pltpu.make_async_copy(whole, whole, own_sem.at[own]).wait()
 
-    def row_part(src, cols):
-        def piece_for(core, side):
-            at = (core * 2 + side) * part_rows
-            return src.at[pl.ds(pl.multiple_of(at, part_rows), part_rows), cols]
-
-        return piece_for
-
     raw_exit, attended_exit, sums_exit = exit_slots(), exit_slots(), exit_slots()
 
     def coefficients():
@@ -591,7 +635,6 @@
     scale = LOG2E * ATT_DIM ** (-0.5)
     ready_kv()
     ready_q()
-    coefficients()
     step_no = 0
     for kv_head in range(kv_heads):
         kv_cols = slice(kv_head * ATT_DIM, (kv_head + 1) * ATT_DIM)
@@ -614,14 +657,22 @@
                 total = jnp.sum(probs, axis=1, keepdims=True)
                 summed = dot(probs.astype(BF16), kv_s[1, seen, kv_cols]) / total
                 for h in range(HEADS_AT_ONCE):
-                    cols = slice(lead + h * ATT_DIM, lead + (h + 1) * ATT_DIM)
-                    attended_s[r : r + tok, cols] = summed[h * tok : (h + 1) * tok].astype(BF16)
+                    part = summed[h * tok : (h + 1) * tok].astype(BF16)
+                    for side in range(2):
+                        owned = part[side * part_rows : (side + 1) * part_rows]
+                        cols = slice(h * ATT_DIM, (h + 1) * ATT_DIM)
+                        attended_s[step_no, r // tok * 2 + side, :, cols] = owned
             size = HEADS_AT_ONCE * ATT_DIM
             at = pl.multiple_of((tp * 2 + parity) * q_all + lead, 128)
             home = attended_out.at[:, pl.ds(at, size)]
-            leave(attended_exit, row_part(attended_s, slice(lead, lead + size)), home)
+            here = attended_s.at[step_no]
+            leave(attended_exit, lambda core, side: here.at[core * 2 + side], home)
+            if step_no == 0:
+                forward()
             for k in range(len(MERGE_AFTER)):
                 if MERGE_AFTER[k] == step_no:
+                    if k == 0:
+                        coefficients()
                     merge(k)
             for k in range(len(PASS_AFTER)):
                 if PASS_AFTER[k] == step_no:
@@ -631,9 +682,9 @@
     ones = jnp.ones((8, 128), F32)
     squares = [jnp.zeros((rows, 128), F32)] * groups
 
-    def finish(local, first):
+    def finish(local, first, count):
         carried = []
-        for k in range(first, first + 2):
+        for k in range(first, first + count):
             if local == 0:
                 carried.append(blend(beside_s, behind_s, k, 4))
             else:
@@ -643,7 +694,7 @@
         incoming = dot(c_s[:, proj], jnp.concatenate(carried, axis=1))
         lead = local * group_width + first * PIECE
         square = squares[local]
-        for tile in range(0, 2 * PIECE, 128):
+        for tile in range(0, count * PIECE, 128):
             cols = slice(lead + tile, lead + tile + 128)
             wide = spread_heads(entry_s[...], cols.start // head_size, head_size)
             z = gate_s[:, cols].astype(F32)
@@ -652,12 +703,19 @@
             square += total * total
             at = parity * width + group_of[local] * group_width + first * PIECE + tile
             gain = weight_ref[:, pl.ds(pl.multiple_of(at, 128), 128)]
-            raw_s[:, cols] = (total * gain).astype(BF16)
+            done = (total * gain).astype(BF16)
+            for rank in range(4):
+                owned = done[rank * part_rows : (rank + 1) * part_rows]
+                raw_s[rank, cols.start // PIECE] = owned
         squares[local] = square
-        at = (tp * 2 + parity) * width + group_of[local] * group_width + first * PIECE
-        home = raw_out.at[:, pl.ds(pl.multiple_of(at, 128), 2 * PIECE)]
-        leave(raw_exit, row_part(raw_s, slice(lead, lead + 2 * PIECE)), home)
-        if first + 2 == pieces:
+        at = ((tp * 2 + parity) * groups + group_of[local]) * pieces + first
+        here = pl.ds(lead // PIECE, count)
+        leave(
+            raw_exit,
+            lambda core, side: raw_s.at[core * 2 + side, here],
+            raw_out.at[pl.ds(at, count)],
+        )
+        if first + count == pieces:
             here = slice(local * 8, local * 8 + 8)
             sums_s[here, :] = dot(ones, square, COLS_LAST, lax.Precision.HIGHEST)
             at = ((tp * 2 + parity) * groups + group_of[local]) * 8
@@ -669,26 +727,42 @@
             leave(sums_exit, half, home)
 
     ready_gate()
-    for k in range(len(MERGE_AFTER), pieces):
-        merge(k)
-    passed = len(PASS_AFTER)
+    merged, passed = len(MERGE_AFTER), len(PASS_AFTER)
     for k in range(0, pieces, 2):
-        while passed < min(pieces, k + 4):
+        while passed < k + 2:
             pass_on(passed)
             passed += 1
-        finish(0, k)
-    for k in range(0, pieces, 2):
-        finish(1, k)
+        finish(0, k, 2)
+        if merged < pieces:
+            merge(merged)
+            merged += 1
+        if passed < pieces:
+            pass_on(passed)
+            passed += 1
+    for k in range(pieces):
+        finish(1, k, 1)
 
     assert used == [send_sem.shape[0], recv_sem.shape[0], own_sem.shape[0]], used
     for close in closing:
         close()
-    for which, step in ((0, 2), (1, 4)):
-
-        @pl.when(reach[step])
-        def _():
-            place = kv_s.at[:, :rows, :]
-            remote(place, place, core_peer, past_send[which], past_recv[0][which]).wait_send()
+    sent = kv_s.at[:, :rows, :]
+
+    @pl.when(ahead)
+    def _():
+        remote(sent, sent, core_peer, past_send[1], past_recv[0][1]).wait_send()
+
+    @pl.when(odd == 0)
+    def _():
+        remote(sent, sent, core_peer, past_send[0], past_recv[0][0]).wait_send()
+
+    @pl.when((odd == 1) & reach[2])
+    def _():
+        part = kv_s.at[:, :rows, :ATT_DIM]
+        remote(part, part, core_peer, past_send[0], past_recv[0][0]).wait_send()
+
+    @pl.when((odd == 1) | ahead)
+    def _():
+        remote(loan_s, loan_s, core_peer, loan_send, loan_recv).wait_send()
 
     half = own_s.at[:pieces]
     remote(half, half, beside, first_send, first_recv).wait_send()
@@ -698,14 +772,14 @@
     def _():
         remote(half, half, beside, merge_send, merge_recv).wait_send()
 
-    settle(attended_exit, attended_s.at[:part_rows, :])
-    settle(raw_exit, raw_s.at[:part_rows, :])
+    settle(attended_exit, attended_s.at[:, 0])
+    settle(raw_exit, raw_s.at[0])
     settle(sums_exit, sums_s.at[:, :tok])
 
 
 def scale_kernel(raw, sums, attended, mixed_out, attended_out, mixed_s, sem):
     tp = lax.axis_index("tp")
-    rows, width = raw.shape
+    rows, width = mixed_s.shape
     group_width = width // GROUPS
     whole = pltpu.make_async_copy(attended, attended_out, sem.at[GROUPS])
     whole.start()
@@ -715,8 +789,10 @@
     factor = lax.rsqrt(squares * (1.0 / group_width) + 1e-05)
     copies = [whole]
     for g in range(GROUPS):
+        for k in range(g * group_width // PIECE, (g + 1) * group_width // PIECE):
+            scaled = raw[k].astype(F32) * factor[:, 8 * g : 8 * g + 1]
+            mixed_s[:, k * PIECE : (k + 1) * PIECE] = scaled.astype(BF16)
         cols = slice(g * group_width, (g + 1) * group_width)
-        mixed_s[:, cols] = (raw[:, cols].astype(F32) * factor[:, 8 * g : 8 * g + 1]).astype(BF16)
         copy = pltpu.make_async_copy(mixed_s.at[:, cols], mixed_out.at[:, cols], sem.at[g])
         copy.start()
         copies.append(copy)
@@ -748,6 +824,7 @@
     vmem_spec = pl.BlockSpec(memory_space=pltpu.VMEM)
     part = rows // 4
     group_pieces = pieces // groups
+    step_width = HEADS_AT_ONCE * ATT_DIM
     state_piece = pltpu.VMEM((group_pieces, state, PIECE), BF16)
     scratch = [
         pltpu.VMEM((rows, half), BF16),
@@ -766,24 +843,25 @@
         pltpu.VMEM((8, 128), F32),
         pltpu.VMEM((8, 128), F32),
         pltpu.VMEM((8, half // groups), F32),
+        pltpu.VMEM((2, rows, kv_half - ATT_DIM), BF16),
         pltpu.VMEM((rows, half), F32),
-        pltpu.VMEM((rows, half), BF16),
+        pltpu.VMEM((4, pieces, part, PIECE), BF16),
         pltpu.VMEM((8 * groups, rows), F32),
-        pltpu.VMEM((rows, q_half), BF16),
+        pltpu.VMEM((q_half // step_width, 4, part, step_width), BF16),
         pltpu.VMEM((rows, 3 * rows), F32),
         pltpu.VMEM((rows, 128), F32),
         pltpu.VMEM((128, rows), F32),
         pltpu.VMEM((128, rows), F32),
         pltpu.VMEM((rows, 128), F32),
         pltpu.VMEM((rows, 128), F32),
-        pltpu.SemaphoreType.DMA((23,)),
-        pltpu.SemaphoreType.DMA((18 + kv_half // ATT_DIM * 2 + 3 * group_pieces,)),
+        pltpu.SemaphoreType.DMA((24,)),
+        pltpu.SemaphoreType.DMA((19 + kv_half // ATT_DIM * 2 + 3 * group_pieces,)),
         pltpu.SemaphoreType.DMA((11,)),
     ]
     raw, sums, attended = pl.pallas_call(
         functools.partial(pair_kernel, lax.axis_size("ctx")),
         out_shape=(
-            pltpu.VMEM((part, 4 * half), BF16),
+            pltpu.VMEM((4 * pieces, part, PIECE), BF16),
             pltpu.VMEM((8 * GROUPS, tok), F32),
             pltpu.VMEM((part, 4 * q_half), BF16),
         ),
@@ -807,12 +885,12 @@
     return pl.pallas_call(
         scale_kernel,
         out_shape=(
-            jax.ShapeDtypeStruct(raw.shape, BF16),
+            jax.ShapeDtypeStruct((part, 4 * half), BF16),
             jax.ShapeDtypeStruct(attended.shape, BF16),
         ),
         in_specs=[vmem_spec] * 3,
         out_specs=(any_spec, any_spec),
-        scratch_shapes=[pltpu.VMEM(raw.shape, BF16), pltpu.SemaphoreType.DMA((GROUPS + 1,))],
+        scratch_shapes=[pltpu.VMEM((part, 4 * half), BF16), pltpu.SemaphoreType.DMA((GROUPS + 1,))],
     )(*[pltpu.with_memory_space_constraint(a, pltpu.VMEM) for a in (raw, sums, attended)])
 
 

time: 40.9 us -> 40.8 us (level); the launches traced: 40.5 us -> 40 us
  Pallas kernels: 39.7 us -> 39.2 us
    pallas_call x1, Pallas kernels: 38.4 us -> 37.8 us  [local_pair(): pl.pallas_call(functools.partial(pair_kernel, lax.axis_size('ctx')), out_...]
where the time goes in v2:
time: 40.8 us; the launch traced here: 40 us
  Pallas kernels  39.2 us (96%)
  between operations  0.8 us (2%)
    pallas_call x1, Pallas kernels, local_pair(): pl.pallas_call(functools.partial(pair_kernel, lax.axis_size('ctx')), out_...  37.8 us
    pallas_call x1, Pallas kernels, local_pair(): pl.pallas_call(scale_kernel, out_shape=(jax.ShapeDtypeStruct((part, 4 * h...  1.39 us

profile of v2, /device:TPU:25, one launch (start us, length us, event | category | flops | bytes accessed | tf_op | source)
XLA Modules:
  0.0 40.0 jit_solution(5421897711512278874)
XLA Ops:
  0.6 37.8 %shard_map.122 = (bf16[64,64,128]{2,1,0:T(8,128)(2,1)S(1)}, f32[64,128]{1,0:T(8,128)S(1)}, bf16[64,8192]{1,0:T(8,128)(2,1)S(1)}) custom-call(s32[32]{0:T(128)} %lengths.1, bf16[128,4096]{1,0:T(8,128)(2,1)} %x_in.1, bf16[128,4096]{1,0:T(8,128)(2,1)} %gate_in.1, bf16[128,1024]{1,0:T(8,128)(2,1)} %b_in.1, bf16[128,1024]{1,0:T(8,128)(2,1)} %c_in.1, ...), custom_call_target="tpu_custom_call" | custom-call | tf_op jit(solution)/shard_map/pallas_call | solution.py:861
  38.5 1.4 %shard_map.123 = (bf16[64,8192]{1,0:T(8,128)(2,1)}, bf16[64,8192]{1,0:T(8,128)(2,1)}) custom-call(bf16[64,64,128]{2,1,0:T(8,128)(2,1)S(1)} %get-tuple-element.5.raw, f32[64,128]{1,0:T(8,128)S(1)} %get-tuple-element.6.sums, bf16[64,8192]{1,0:T(8,128)(2,1)S(1)} %get-tuple-element.7.attended), custom_call_target="tpu_custom_call" | custom-call | tf_op jit(solution)/shard_map/pallas_call | solution.py:885

commit v3 on v2

--- a/solution.py
+++ b/solution.py
@@ -198,8 +198,8 @@
 ROWS_FIRST = (((0,), (0,)), ((), ()))
 PIECE = 128
 HEADS_AT_ONCE = 2
-MERGE_AFTER = (1, 2, 3, 5, 6, 7)
-PASS_AFTER = (4, 5, 7)
+MERGE_AFTER = (3, 5)
+PASS_AFTER = (7,)
 
 
 def dot(a, b, dims=(((1,), (0,)), ((), ())), precision=None):
@@ -287,21 +287,25 @@
     cross_peer = (base + other, 1 - tp)
     beside = (index + 2 - 4 * odd, tp)
     barrier = pltpu.get_barrier_semaphore()
+    ahead, behind = base + 4 < n, base >= 4
+    fed = (odd == 1) | behind
+    feeds = (odd == 0) | behind
     greeted = jnp.int32(3)
-    reach = {}
+
+    def greet(peer):
+        pl.semaphore_signal(barrier, inc=1, device_id=peer, device_id_type=MESH_ID)
+
     for step in (2, 4, -2, -4):
-        reach[step] = (base + step >= 0) & (base + step < n)
-        greeted += 2 * reach[step].astype(jnp.int32)
-
-        @pl.when(reach[step])
+        there = (base + step >= 0) & (base + step < n)
+        greeted += 2 * there.astype(jnp.int32)
+
+        @pl.when(there)
         def _():
             for core in range(2):
-                peer = (base + step + core, tp)
-                pl.semaphore_signal(barrier, inc=1, device_id=peer, device_id_type=MESH_ID)
+                greet((base + step + core, tp))
 
     for peer in (core_peer, tp_peer, cross_peer):
-        pl.semaphore_signal(barrier, inc=1, device_id=peer, device_id_type=MESH_ID)
-    ahead, behind = reach[4], reach[-4]
+        greet(peer)
 
     used = [0, 0, 0]
 
@@ -321,20 +325,19 @@
 
     at_mine = pl.multiple_of(parity * tok, tok)
     mine = pl.ds(at_mine, tok)
-    closing = []
-
-    def trade(moves, whole):
-        send, recv, own = slots(0), slots(1), slots(2)
+
+    trade_send, trade_own = slots(0), slots(2)
+    step_send, step_own = slots(0), slots(2)
+
+    def trade(moves, whole, recv, send=trade_send, own=trade_own):
         for give, keep, place in moves:
             pltpu.make_async_copy(keep, place, own_sem.at[own]).start()
-        closing.append(remote(whole, whole, core_peer, send, recv).wait_send)
 
         def start():
             for give, keep, place in moves:
                 remote(give, place, core_peer, send, recv).start()
 
         def ready():
-            pltpu.make_async_copy(whole, whole, own_sem.at[own]).wait()
             remote(whole, whole, core_peer, send, recv).wait_recv()
 
         return start, ready
@@ -350,7 +353,8 @@
         for local in local_groups:
             place = dst.at[mine, local * size : (local + 1) * size]
             moves.append((part(other, local), part(parity, local), place))
-        return trade(moves, dst.at[:tok, first * size : (first + len(local_groups)) * size])
+        whole = dst.at[:tok, first * size : (first + len(local_groups)) * size]
+        return trade(moves, whole, slots(1))
 
     def part_of(src, core, begin, size, total):
         return src.at[:, pl.ds(pl.multiple_of(core * total + begin, 128), size)]
@@ -362,64 +366,90 @@
     @pl.when(pair < 1)
     def _():
         kv_s[:, rows : 2 * rows, :] = jnp.zeros((2, rows, kv_width), BF16)
-
-    past_send = (slots(0), slots(0))
-    past_recv = [(slots(1), slots(1)) for head in range(kv_heads)]
-    loan_send, loan_recv = slots(0), slots(1)
+        second_s[...] = jnp.zeros_like(second_s)
+
+    @pl.when((odd == 0) & jnp.logical_not(ahead))
+    def _():
+        beside_s[...] = jnp.zeros_like(beside_s)
+
+    near_send, far_send = slots(0), slots(0)
+    near_recv = [slots(1) for head in range(kv_heads)]
+    far_recv = [slots(1) for head in range(kv_heads)]
+    early = base + 8 < n
+    items = []
+    for head in range(1, kv_heads):
+        items += [(0, head, early), (1, head, early & ((base + 12 < n) | (base < 4)))]
+    item_send, loan_recv = slots(0, len(items)), slots(1, len(items))
 
     def head_cols(head):
         return slice(head * ATT_DIM, (head + 1) * ATT_DIM)
 
-    def send_past(head, dst, step, skip, which, recv):
-        for k, src in enumerate((k_in, v_in)):
-            for core in range(2):
-                remote(
-                    part_of(src, core, head * ATT_DIM, ATT_DIM, kv_width),
-                    dst.at[k, pl.ds(at_mine + skip, tok), :],
-                    (base + step + core, tp),
-                    which,
-                    recv,
-                ).start()
-
-    def send_near(head):
-        near = kv_s.at[:, :, head_cols(head)]
-
-        @pl.when(reach[2] & ((odd == 0) | (head == 0)))
-        def _():
-            send_past(head, near, 2, rows, past_send[0], past_recv[head][0])
-
-    def lend():
-        @pl.when(odd == 1)
-        def _():
-            for head in range(1, kv_heads):
-                send_past(head, loan_s.at[:, :, head_cols(head - 1)], -2, 0, loan_send, loan_recv)
-
-    def send_far(head):
-        @pl.when(reach[4])
-        def _():
-            far = kv_s.at[:, :, head_cols(head)]
-            send_past(head, far, 4, 0, past_send[1], past_recv[head][1])
-
-    def near_loan():
-        return kv_s.at[:, rows : 2 * rows, ATT_DIM:]
-
-    def forward():
+    def send_part(k, head, dst, step, skip, send, recv):
+        for core in range(2):
+            remote(
+                part_of((k_in, v_in)[k], core, head * ATT_DIM, ATT_DIM, kv_width),
+                dst.at[pl.ds(at_mine + skip, tok), :],
+                (base + step + core, tp),
+                send,
+                recv,
+            ).start()
+
+    def send_near():
         @pl.when(odd == 0)
         def _():
-            remote(loan_s, loan_s, core_peer, loan_send, loan_recv).wait_recv()
-
-        @pl.when((odd == 0) & ahead)
+            for head in range(kv_heads):
+                for k in range(2):
+                    near = kv_s.at[k, :, head_cols(head)]
+                    send_part(k, head, near, 2, rows, near_send, near_recv[head])
+
+        @pl.when((odd == 1) & ahead)
         def _():
-            peer = (index + 4, tp)
-            remote(loan_s, near_loan(), peer, loan_send, past_recv[1][0]).start()
+            for k in range(2):
+                near = kv_s.at[k, :, head_cols(0)]
+                send_part(k, 0, near, 2, rows, near_send, near_recv[0])
+
+        for j, (k, head, lent) in enumerate(items):
+
+            @pl.when((odd == 1) & lent)
+            def _():
+                send_part(k, head, loan_s.at[j], -2, 0, item_send + j, loan_recv + j)
+
+    def send_rest():
+        for j, (k, head, lent) in enumerate(items):
+
+            @pl.when((odd == 1) & ahead & jnp.logical_not(lent))
+            def _():
+                near = kv_s.at[k, :, head_cols(head)]
+                send_part(k, head, near, 2, rows, item_send + j, near_recv[head])
+
+    def send_far(head):
+        @pl.when(ahead)
+        def _():
+            for k in range(2):
+                far = kv_s.at[k, :, head_cols(head)]
+                send_part(k, head, far, 4, 0, far_send, far_recv[head])
+
+    def arrived(place, recv):
+        remote(place, place, core_peer, far_send, recv).wait_recv()
+
+    def forward():
+        for j, (k, head, lent) in enumerate(items):
+
+            @pl.when((odd == 0) & lent)
+            def _():
+                arrived(loan_s.at[j], loan_recv + j)
+                near = kv_s.at[k, rows : 2 * rows, head_cols(head)]
+                peer = (index + 4, tp)
+                remote(loan_s.at[j], near, peer, item_send + j, near_recv[head]).start()
 
     def wait_past(head):
-        for which, step, skip in ((0, -2, rows), (1, -4, 0)):
-
-            @pl.when(reach[step])
-            def _():
-                place = kv_s.at[:, skip : skip + rows, head_cols(head)]
-                remote(place, place, core_peer, past_send[which], past_recv[head][which]).wait_recv()
+        @pl.when(fed)
+        def _():
+            arrived(kv_s.at[:, rows : 2 * rows, head_cols(head)], near_recv[head])
+
+        @pl.when(behind)
+        def _():
+            arrived(kv_s.at[:, :rows, head_cols(head)], far_recv[head])
 
     moves = []
     for local in range(groups):
@@ -430,7 +460,7 @@
             return step_in.at[pl.ds(pl.multiple_of(at, 8), group_heads)]
 
         moves.append((step_part(other), step_part(parity), place))
-    start_step, ready_step = trade(moves, step_s.at[:, :tok])
+    start_step, ready_step = trade(moves, step_s.at[:, :tok], slots(1), step_send, step_own)
     start_b, ready_b = by_group(b_in, b_s, tuple(range(groups)))
     trade_x = {local: by_group(x_in, x_s, (local,)) for local in (1, 0)}
     start_c, ready_c = by_group(c_in, c_s, tuple(range(groups)))
@@ -439,10 +469,11 @@
         give = part_of(src, other, 0, kv_width, kv_width)
         keep = part_of(src, parity, 0, kv_width, kv_width)
         moves.append((give, keep, kv_s.at[k, pl.ds(at_mine + 2 * rows, tok), :]))
-    start_kv, ready_kv = trade(moves, kv_s.at[:, 2 * rows : 2 * rows + tok, :])
+    ready_kvq = slots(1)
+    start_kv, _ = trade(moves, kv_s.at[:, :tok, :], ready_kvq)
     q_all = q_s.shape[1]
     give, keep = part_of(q_in, other, 0, q_all, q_all), part_of(q_in, parity, 0, q_all, q_all)
-    start_q, ready_q = trade([(give, keep, q_s.at[mine, :])], q_s.at[:tok, :])
+    start_q, _ = trade([(give, keep, q_s.at[mine, :])], q_s.at[:tok, :], ready_kvq)
     start_gate, ready_gate = by_group(gate_in, gate_s, tuple(range(groups)))
 
     @pl.when(pair < 2)
@@ -464,19 +495,17 @@
     bias_s[...] = jnp.where((row_doc == col_doc) & (row_at <= col_at), 0.0, NEG_LARGE)
 
     pl.semaphore_wait(barrier, greeted)
-    send_near(0)
+    send_near()
     start_step()
     start_b()
     send_far(0)
     for local in (1, 0):
         trade_x[local][0]()
-    for head in range(1, kv_heads):
-        send_near(head)
-        send_far(head)
     for start in (start_c, start_kv, start_q, start_gate):
         start()
 
     ready_step()
+    pltpu.make_async_copy(step_s.at[:, :tok], step_s.at[:, :tok], own_sem.at[step_own]).wait()
     step_t = jnp.concatenate([step_s[...], jnp.zeros((128 - heads, rows), F32)], axis=0)
     step = step_t.T
     rates = []
@@ -509,27 +538,38 @@
     t_own[...] = jnp.broadcast_to(jnp.exp(final_sum) * passing, t_own.shape)
     t_trip = remote(t_own, t_beside, beside, slots(0), slots(1))
     t_trip.start()
-    closing.append(t_trip.wait_send)
-
-    first_send, first_recv = slots(0), slots(1, pieces)
-    merge_send, merge_recv = slots(0), slots(1, pieces)
-    pass_send, pass_recv = slots(0), slots(1, pieces)
+
+    pairs = pieces // 2
+    first_send, first_recv = slots(0), slots(1, pairs)
+    merge_send, merge_recv = slots(0), slots(1, pairs)
+    pass_send, pass_recv = slots(0), slots(1, pairs + 1)
+
+    def two(k):
+        return slice(2 * k, 2 * k + 2)
 
     def first_trip(k):
-        return remote(
-            own_s.at[pieces + k], beside_s.at[k], beside, first_send, first_recv + k
-        )
+        src = own_s.at[pieces + 2 * k : pieces + 2 * k + 2]
+        return remote(src, beside_s.at[two(k)], beside, first_send, first_recv + k)
 
     def merge_trip(k):
-        return remote(
-            merged_s.at[k], behind_s.at[k], (index + 4, tp), merge_send, merge_recv + k
-        )
-
-    def pass_trip(k):
-        return remote(passed_s.at[k], second_s.at[k], beside, pass_send, pass_recv + k)
+        src, peer = merged_s.at[two(k)], (index + 4, tp)
+        return remote(src, behind_s.at[two(k)], peer, merge_send, merge_recv + k)
+
+    def pass_trip(begin, count):
+        span = slice(begin, begin + count)
+        recv = pass_recv + (begin // 2 if count == 2 else begin - pieces + pairs + 1)
+        return remote(passed_s.at[span], second_s.at[span], beside, pass_send, recv)
+
+    def pass_trips(k):
+        if k < pairs - 1:
+            return [pass_trip(2 * k, 2)]
+        return [pass_trip(2 * k, 1), pass_trip(2 * k + 1, 1)]
+
+    traded = 2 * groups * state // 128 + 2 * width // 128 + q_all // 128 + 2 * kv_width // 128
+    traded_ref = y_s.at[: traded * tok * 128 * 2 // (width * 4)]
 
     per = 128 // head_size
-    lend()
+    pltpu.make_async_copy(traded_ref, traded_ref, own_sem.at[trade_own]).wait()
     ready_b()
     for local in (1, 0):
         trade_x[local][1]()
@@ -543,9 +583,16 @@
             made = dot(b_t, jnp.concatenate(parts, axis=1)).astype(BF16)
             for tile in range(2):
                 own_s[k + tile] = made[:, tile * PIECE : (tile + 1) * PIECE]
-                if local == 1:
-                    first_trip(k + tile - pieces).start()
-
+        if local == 1:
+
+            @pl.when((odd == 0) | ahead)
+            def _():
+                for k in range(pairs):
+                    first_trip(k).start()
+
+    for head in range(1, kv_heads):
+        send_far(head)
+    send_rest()
     ready_c()
     for g in range(groups):
         proj = slice(g * state, (g + 1) * state)
@@ -571,23 +618,18 @@
     part_rows = rows // 4
     exits = ((tp_peer, 0, 1), (cross_peer, 1, 1), (core_peer, 1, 0))
 
-    def exit_slots():
-        return slots(0, 3), slots(1, 3), slots(2)
-
-    def leave(sems, piece_for, home):
-        send, recv, own = sems
-        for k, (peer, far_core, far_tp) in enumerate(exits):
+    exit_send, exit_recv, exit_own = slots(0), slots(1), slots(2)
+    sums_send, sums_recv, sums_own = slots(0), slots(1), slots(2)
+
+    def leave(piece_for, home, send=exit_send, recv=exit_recv, own=exit_own):
+        for peer, far_core, far_tp in exits:
             src = piece_for(other if far_core else parity, 1 - tp if far_tp else tp)
-            remote(src, home, peer, send + k, recv + k).start()
+            remote(src, home, peer, send, recv).start()
         pltpu.make_async_copy(piece_for(parity, tp), home, own_sem.at[own]).start()
 
-    def settle(sems, whole):
-        send, recv, own = sems
-        for k, (peer, far_core, far_tp) in enumerate(exits):
-            remote(whole, whole, peer, send + k, recv + k).wait()
-        pltpu.make_async_copy(whole, whole, own_sem.at[own]).wait()
-
-    raw_exit, attended_exit, sums_exit = exit_slots(), exit_slots(), exit_slots()
+    def settle(thrice, once, send, recv, own):
+        remote(thrice, thrice, core_peer, send, recv).wait()
+        pltpu.make_async_copy(once, once, own_sem.at[own]).wait()
 
     def coefficients():
         t_trip.wait_recv()
@@ -617,8 +659,9 @@
         return total.astype(BF16)
 
     def merge(k):
-        first_trip(k).wait_recv()
-        merged_s[k] = blend(beside_s, own_s, k, 0)
+        pl.when((odd == 1) | ahead)(first_trip(k).wait_recv)
+        for j in (2 * k, 2 * k + 1):
+            merged_s[j] = blend(beside_s, own_s, j, 0)
 
         @pl.when(ahead)
         def _():
@@ -629,12 +672,16 @@
         def _():
             merge_trip(k).wait_recv()
 
-        passed_s[k] = blend(own_s, behind_s, k, 2)
-        pass_trip(k).start()
+        @pl.when(feeds)
+        def _():
+            for j in (2 * k, 2 * k + 1):
+                passed_s[j] = blend(own_s, behind_s, j, 2)
+            for trip in pass_trips(k):
+                trip.start()
 
     scale = LOG2E * ATT_DIM ** (-0.5)
-    ready_kv()
-    ready_q()
+    kvq = y_s.at[: (2 * kv_width + q_all) * tok * 2 // (width * 4)]
+    arrived(kvq, ready_kvq)
     step_no = 0
     for kv_head in range(kv_heads):
         kv_cols = slice(kv_head * ATT_DIM, (kv_head + 1) * ATT_DIM)
@@ -666,7 +713,7 @@
             at = pl.multiple_of((tp * 2 + parity) * q_all + lead, 128)
             home = attended_out.at[:, pl.ds(at, size)]
             here = attended_s.at[step_no]
-            leave(attended_exit, lambda core, side: here.at[core * 2 + side], home)
+            leave(lambda core, side: here.at[core * 2 + side], home)
             if step_no == 0:
                 forward()
             for k in range(len(MERGE_AFTER)):
@@ -679,27 +726,30 @@
                     pass_on(k)
             step_no += 1
 
-    ones = jnp.ones((8, 128), F32)
+    ones = jnp.ones((8, 256), BF16)
     squares = [jnp.zeros((rows, 128), F32)] * groups
 
     def finish(local, first, count):
-        carried = []
-        for k in range(first, first + count):
-            if local == 0:
-                carried.append(blend(beside_s, behind_s, k, 4))
-            else:
-                pass_trip(k).wait_recv()
-                carried.append(second_s[k])
-        proj = slice(local * state, (local + 1) * state)
-        incoming = dot(c_s[:, proj], jnp.concatenate(carried, axis=1))
         lead = local * group_width + first * PIECE
-        square = squares[local]
+        ready, fed_by = [], []
         for tile in range(0, count * PIECE, 128):
             cols = slice(lead + tile, lead + tile + 128)
             wide = spread_heads(entry_s[...], cols.start // head_size, head_size)
             z = gate_s[:, cols].astype(F32)
-            total = y_s[:, cols] + incoming[:, tile : tile + 128] * wide
-            total = total * (z / (1.0 + jnp.exp(-z)))
+            z = z / (1.0 + jnp.exp(-z))
+            ready.append(y_s[:, cols] * z)
+            fed_by.append(wide * z)
+        if local == 1:
+            pl.when(fed)(pass_trip(first, count).wait_recv)
+        carried = []
+        for k in range(first, first + count):
+            carried.append(blend(beside_s, behind_s, k, 4) if local == 0 else second_s[k])
+        proj = slice(local * state, (local + 1) * state)
+        incoming = dot(c_s[:, proj], jnp.concatenate(carried, axis=1))
+        square = squares[local]
+        for tile in range(0, count * PIECE, 128):
+            cols = slice(lead + tile, lead + tile + 128)
+            total = ready[tile // 128] + incoming[:, tile : tile + 128] * fed_by[tile // 128]
             square += total * total
             at = parity * width + group_of[local] * group_width + first * PIECE + tile
             gain = weight_ref[:, pl.ds(pl.multiple_of(at, 128), 128)]
@@ -711,83 +761,93 @@
         at = ((tp * 2 + parity) * groups + group_of[local]) * pieces + first
         here = pl.ds(lead // PIECE, count)
         leave(
-            raw_exit,
             lambda core, side: raw_s.at[core * 2 + side, here],
             raw_out.at[pl.ds(at, count)],
         )
         if first + count == pieces:
             here = slice(local * 8, local * 8 + 8)
-            sums_s[here, :] = dot(ones, square, COLS_LAST, lax.Precision.HIGHEST)
+            high = square.astype(BF16)
+            halves = [high, (square - high.astype(F32)).astype(BF16)]
+            sums_s[here, :] = dot(ones, jnp.concatenate(halves, axis=1), COLS_LAST)
             at = ((tp * 2 + parity) * groups + group_of[local]) * 8
             home = sums_out.at[pl.ds(pl.multiple_of(at, 8), 8), :]
 
             def half(core, side):
                 return sums_s.at[here, pl.ds(pl.multiple_of(core * tok, tok), tok)]
 
-            leave(sums_exit, half, home)
+            leave(half, home, sums_send, sums_recv, sums_own)
 
     ready_gate()
     merged, passed = len(MERGE_AFTER), len(PASS_AFTER)
-    for k in range(0, pieces, 2):
-        while passed < k + 2:
+    for k in range(pairs):
+        while passed <= k:
             pass_on(passed)
             passed += 1
-        finish(0, k, 2)
-        if merged < pieces:
+        finish(0, 2 * k, 2)
+        while merged < pairs:
             merge(merged)
             merged += 1
-        if passed < pieces:
-            pass_on(passed)
-            passed += 1
-    for k in range(pieces):
-        finish(1, k, 1)
+    for k in range(pairs - 1):
+        finish(1, 2 * k, 2)
+    finish(1, pieces - 2, 1)
+    finish(1, pieces - 1, 1)
 
     assert used == [send_sem.shape[0], recv_sem.shape[0], own_sem.shape[0]], used
-    for close in closing:
-        close()
+    t_trip.wait_send()
+    remote(traded_ref, traded_ref, core_peer, trade_send, loan_recv).wait_send()
+    given = step_s.at[:, :tok]
+    remote(given, given, core_peer, step_send, loan_recv).wait_send()
     sent = kv_s.at[:, :rows, :]
 
     @pl.when(ahead)
     def _():
-        remote(sent, sent, core_peer, past_send[1], past_recv[0][1]).wait_send()
+        remote(sent, sent, core_peer, far_send, loan_recv).wait_send()
+
+    for j, (k, head, lent) in enumerate(items):
+
+        @pl.when(lent | ((odd == 1) & ahead))
+        def _():
+            remote(loan_s.at[j], loan_s.at[j], core_peer, item_send + j, loan_recv).wait_send()
 
     @pl.when(odd == 0)
     def _():
-        remote(sent, sent, core_peer, past_send[0], past_recv[0][0]).wait_send()
-
-    @pl.when((odd == 1) & reach[2])
+        remote(sent, sent, core_peer, near_send, loan_recv).wait_send()
+
+    @pl.when((odd == 1) & ahead)
     def _():
-        part = kv_s.at[:, :rows, :ATT_DIM]
-        remote(part, part, core_peer, past_send[0], past_recv[0][0]).wait_send()
-
-    @pl.when((odd == 1) | ahead)
-    def _():
-        remote(loan_s, loan_s, core_peer, loan_send, loan_recv).wait_send()
+        part = kv_s.at[:, :rows, head_cols(0)]
+        remote(part, part, core_peer, near_send, loan_recv).wait_send()
 
     half = own_s.at[:pieces]
-    remote(half, half, beside, first_send, first_recv).wait_send()
-    remote(half, half, beside, pass_send, pass_recv).wait_send()
+    pl.when((odd == 0) | ahead)(remote(half, half, beside, first_send, first_recv).wait_send)
+    pl.when(feeds)(remote(half, half, beside, pass_send, pass_recv).wait_send)
 
     @pl.when(ahead)
     def _():
         remote(half, half, beside, merge_send, merge_recv).wait_send()
 
-    settle(attended_exit, attended_s.at[:, 0])
-    settle(raw_exit, raw_s.at[0])
-    settle(sums_exit, sums_s.at[:, :tok])
+    left = (width + q_all) * part_rows * 2 // (width * 4)
+    settle(y_s.at[: 3 * left], y_s.at[:left], exit_send, exit_recv, exit_own)
+    left = 8 * groups
+    settle(l_s.at[: 3 * left], l_s.at[:left], sums_send, sums_recv, sums_own)
 
 
 def scale_kernel(raw, sums, attended, mixed_out, attended_out, mixed_s, sem):
     tp = lax.axis_index("tp")
     rows, width = mixed_s.shape
     group_width = width // GROUPS
-    whole = pltpu.make_async_copy(attended, attended_out, sem.at[GROUPS])
-    whole.start()
+    copies = []
+    for k in range(0, rows, 16):
+        part = slice(k, k + 16)
+        copy = pltpu.make_async_copy(
+            attended.at[part], attended_out.at[part], sem.at[GROUPS + k // 16]
+        )
+        copy.start()
+        copies.append(copy)
     squares = sums[...]
     squares = jnp.concatenate([squares, jnp.zeros((128 - squares.shape[0], 128), F32)], axis=0).T
     squares = jnp.where(tp == 0, squares[:rows], squares[rows:])
     factor = lax.rsqrt(squares * (1.0 / group_width) + 1e-05)
-    copies = [whole]
     for g in range(GROUPS):
         for k in range(g * group_width // PIECE, (g + 1) * group_width // PIECE):
             scaled = raw[k].astype(F32) * factor[:, 8 * g : 8 * g + 1]
@@ -824,6 +884,7 @@
     vmem_spec = pl.BlockSpec(memory_space=pltpu.VMEM)
     part = rows // 4
     group_pieces = pieces // groups
+    items = 2 * kv_half // ATT_DIM - 2
     step_width = HEADS_AT_ONCE * ATT_DIM
     state_piece = pltpu.VMEM((group_pieces, state, PIECE), BF16)
     scratch = [
@@ -843,7 +904,7 @@
         pltpu.VMEM((8, 128), F32),
         pltpu.VMEM((8, 128), F32),
         pltpu.VMEM((8, half // groups), F32),
-        pltpu.VMEM((2, rows, kv_half - ATT_DIM), BF16),
+        pltpu.VMEM((items, rows, ATT_DIM), BF16),
         pltpu.VMEM((rows, half), F32),
         pltpu.VMEM((4, pieces, part, PIECE), BF16),
         pltpu.VMEM((8 * groups, rows), F32),
@@ -854,9 +915,9 @@
         pltpu.VMEM((128, rows), F32),
         pltpu.VMEM((rows, 128), F32),
         pltpu.VMEM((rows, 128), F32),
-        pltpu.SemaphoreType.DMA((24,)),
-        pltpu.SemaphoreType.DMA((19 + kv_half // ATT_DIM * 2 + 3 * group_pieces,)),
-        pltpu.SemaphoreType.DMA((11,)),
+        pltpu.SemaphoreType.DMA((10 + items,)),
+        pltpu.SemaphoreType.DMA((11 + kv_half // ATT_DIM * 2 + items + 3 * group_pieces // 2,)),
+        pltpu.SemaphoreType.DMA((4,)),
     ]
     raw, sums, attended = pl.pallas_call(
         functools.partial(pair_kernel, lax.axis_size("ctx")),
@@ -890,7 +951,7 @@
         ),
         in_specs=[vmem_spec] * 3,
         out_specs=(any_spec, any_spec),
-        scratch_shapes=[pltpu.VMEM((part, 4 * half), BF16), pltpu.SemaphoreType.DMA((GROUPS + 1,))],
+        scratch_shapes=[pltpu.VMEM((part, 4 * half), BF16), pltpu.SemaphoreType.DMA((GROUPS + part // 16,))],
     )(*[pltpu.with_memory_space_constraint(a, pltpu.VMEM) for a in (raw, sums, attended)])
 
 

time: 40.8 us -> 39.9 us (0.978)
  Pallas kernels: 39.2 us -> 38.6 us
    pallas_call x1, Pallas kernels: 37.8 us -> 37.2 us  [local_pair(): pl.pallas_call(functools.partial(pair_kernel, lax.axis_size('ctx')), out_...]
where the time goes in v3:
time: 39.9 us; the launch traced here: 39.4 us
  Pallas kernels  38.6 us (97%)
  between operations  0.8 us (2%)
    pallas_call x1, Pallas kernels, local_pair(): pl.pallas_call(functools.partial(pair_kernel, lax.axis_size('ctx')), out_...  37.2 us
    pallas_call x1, Pallas kernels, local_pair(): pl.pallas_call(scale_kernel, out_shape=(jax.ShapeDtypeStruct((part, 4 * h...  1.41 us

profile of v3, /device:TPU:25, one launch (start us, length us, event | category | flops | bytes accessed | tf_op | source)
XLA Modules:
  0.0 39.4 jit_solution(2190760023316743522)
XLA Ops:
  0.6 37.2 %shard_map.122 = (bf16[64,64,128]{2,1,0:T(8,128)(2,1)S(1)}, f32[64,128]{1,0:T(8,128)S(1)}, bf16[64,8192]{1,0:T(8,128)(2,1)S(1)}) custom-call(s32[32]{0:T(128)} %lengths.1, bf16[128,4096]{1,0:T(8,128)(2,1)} %x_in.1, bf16[128,4096]{1,0:T(8,128)(2,1)} %gate_in.1, bf16[128,1024]{1,0:T(8,128)(2,1)} %b_in.1, bf16[128,1024]{1,0:T(8,128)(2,1)} %c_in.1, ...), custom_call_target="tpu_custom_call" | custom-call | tf_op jit(solution)/shard_map/pallas_call | solution.py:922
  37.8 1.4 %shard_map.123 = (bf16[64,8192]{1,0:T(8,128)(2,1)}, bf16[64,8192]{1,0:T(8,128)(2,1)}) custom-call(bf16[64,64,128]{2,1,0:T(8,128)(2,1)S(1)} %get-tuple-element.5.raw, f32[64,128]{1,0:T(8,128)S(1)} %get-tuple-element.6.sums, bf16[64,8192]{1,0:T(8,128)(2,1)S(1)} %get-tuple-element.7.attended), custom_call_target="tpu_custom_call" | custom-call | tf_op jit(solution)/shard_map/pallas_call | solution.py:946

commit v4 on v3

--- a/solution.py
+++ b/solution.py
@@ -216,7 +216,7 @@
 
 def pair_kernel(
     n,
-    lengths,
+    lengths_in,
     x_in,
     gate_in,
     b_in,
@@ -225,8 +225,8 @@
     q_in,
     k_in,
     v_in,
-    rate_ref,
-    weight_ref,
+    rate_in,
+    weight_in,
     raw_out,
     sums_out,
     attended_out,
@@ -247,6 +247,9 @@
     t_beside,
     coef_s,
     loan_s,
+    lengths,
+    rate_ref,
+    weight_ref,
     y_s,
     raw_s,
     sums_s,
@@ -307,7 +310,11 @@
     for peer in (core_peer, tp_peer, cross_peer):
         greet(peer)
 
-    used = [0, 0, 0]
+    small = ((lengths_in, lengths), (rate_in, rate_ref), (weight_in, weight_ref))
+    small = [pltpu.make_async_copy(src, dst, own_sem.at[k]) for k, (src, dst) in enumerate(small)]
+    for copy in small:
+        copy.start()
+    used = [0, 0, len(small)]
 
     def slots(kind, count=1):
         used[kind] += count
@@ -480,6 +487,7 @@
     def _():
         behind_s[...] = jnp.zeros_like(behind_s)
 
+    small[0].wait()
     begin = pair * rows
     row_at = begin - 2 * rows + lax.broadcasted_iota(jnp.int32, (1, 3 * rows), 1)
     col_at = begin + lax.broadcasted_iota(jnp.int32, (rows, 1), 0)
@@ -504,6 +512,8 @@
     for start in (start_c, start_kv, start_q, start_gate):
         start()
 
+    small[1].wait()
+    small[2].wait()
     ready_step()
     pltpu.make_async_copy(step_s.at[:, :tok], step_s.at[:, :tok], own_sem.at[step_own]).wait()
     step_t = jnp.concatenate([step_s[...], jnp.zeros((128 - heads, rows), F32)], axis=0)
@@ -590,30 +600,32 @@
                 for k in range(pairs):
                     first_trip(k).start()
 
+    send_rest()
     for head in range(1, kv_heads):
         send_far(head)
-    send_rest()
     ready_c()
-    for g in range(groups):
-        proj = slice(g * state, (g + 1) * state)
-        inter = dot(c_s[:, proj], b_s[:, proj], COLS_LAST)
-        for tile in range(group_width // 128):
-            lead = g * group_width + tile * 128
-            halves = []
-            for r in range(0, rows, tok):
-                seen = slice(0, r + tok)
-                bias = bias_s[r : r + tok, 2 * rows : 2 * rows + r + tok]
-                mixing = []
-                for h in range(lead // head_size, lead // head_size + per):
-                    spread = l_s[r : r + tok, h : h + 1] - lt_s[h : h + 1, seen]
-                    w = jnp.exp(spread + bias) * dtt_s[h : h + 1, seen] * inter[r : r + tok, seen]
-                    mixing.append(w.astype(BF16))
-                both = dot(jnp.concatenate(mixing, axis=0), x_s[seen, lead : lead + 128])
-                whole = both[:tok]
-                for k in range(1, per):
-                    part = both[k * tok : (k + 1) * tok]
-                    whole = jnp.where(lane[:tok] >= k * head_size, part, whole)
-                y_s[r : r + tok, lead : lead + 128] = whole
+
+    def intra():
+        for g in range(groups):
+            proj = slice(g * state, (g + 1) * state)
+            inter = dot(c_s[:, proj], b_s[:, proj], COLS_LAST)
+            for tile in range(group_width // 128):
+                lead = g * group_width + tile * 128
+                halves = []
+                for r in range(0, rows, tok):
+                    seen = slice(0, r + tok)
+                    bias = bias_s[r : r + tok, 2 * rows : 2 * rows + r + tok]
+                    mixing = []
+                    for h in range(lead // head_size, lead // head_size + per):
+                        spread = l_s[r : r + tok, h : h + 1] - lt_s[h : h + 1, seen]
+                        w = jnp.exp(spread + bias) * dtt_s[h : h + 1, seen] * inter[r : r + tok, seen]
+                        mixing.append(w.astype(BF16))
+                    both = dot(jnp.concatenate(mixing, axis=0), x_s[seen, lead : lead + 128])
+                    whole = both[:tok]
+                    for k in range(1, per):
+                        part = both[k * tok : (k + 1) * tok]
+                        whole = jnp.where(lane[:tok] >= k * head_size, part, whole)
+                    y_s[r : r + tok, lead : lead + 128] = whole
 
     part_rows = rows // 4
     exits = ((tp_peer, 0, 1), (cross_peer, 1, 1), (core_peer, 1, 0))
@@ -682,8 +694,8 @@
     scale = LOG2E * ATT_DIM ** (-0.5)
     kvq = y_s.at[: (2 * kv_width + q_all) * tok * 2 // (width * 4)]
     arrived(kvq, ready_kvq)
-    step_no = 0
-    for kv_head in range(kv_heads):
+    def attend(kv_head):
+        step_no = kv_head * q_width // (HEADS_AT_ONCE * ATT_DIM)
         kv_cols = slice(kv_head * ATT_DIM, (kv_head + 1) * ATT_DIM)
         wait_past(kv_head)
         for lead in range(kv_head * q_width, (kv_head + 1) * q_width, HEADS_AT_ONCE * ATT_DIM):
@@ -725,6 +737,15 @@
                 if PASS_AFTER[k] == step_no:
                     pass_on(k)
             step_no += 1
+
+    @pl.loop(0, 2)
+    def _(turn):
+        attend_now = lax.rem(turn + (pair == 0).astype(jnp.int32), 2) == 1
+        pl.when(attend_now)(functools.partial(attend, 0))
+        pl.when(jnp.logical_not(attend_now))(intra)
+
+    for kv_head in range(1, kv_heads):
+        attend(kv_head)
 
     ones = jnp.ones((8, 256), BF16)
     squares = [jnp.zeros((rows, 128), F32)] * groups
@@ -780,6 +801,8 @@
     ready_gate()
     merged, passed = len(MERGE_AFTER), len(PASS_AFTER)
     for k in range(pairs):
+        if k == 2:
+            finish(1, 0, 2)
         while passed <= k:
             pass_on(passed)
             passed += 1
@@ -787,7 +810,7 @@
         while merged < pairs:
             merge(merged)
             merged += 1
-    for k in range(pairs - 1):
+    for k in range(1, pairs - 1):
         finish(1, 2 * k, 2)
     finish(1, pieces - 2, 1)
     finish(1, pieces - 1, 1)
@@ -905,6 +928,9 @@
         pltpu.VMEM((8, 128), F32),
         pltpu.VMEM((8, half // groups), F32),
         pltpu.VMEM((items, rows, ATT_DIM), BF16),
+        pltpu.SMEM(doc_lengths.shape, jnp.int32),
+        pltpu.VMEM((1, decay_rate.shape[0]), F32),
+        pltpu.VMEM((1, norm_weight.shape[0]), F32),
         pltpu.VMEM((rows, half), F32),
         pltpu.VMEM((4, pieces, part, PIECE), BF16),
         pltpu.VMEM((8 * groups, rows), F32),
@@ -917,7 +943,7 @@
         pltpu.VMEM((rows, 128), F32),
         pltpu.SemaphoreType.DMA((10 + items,)),
         pltpu.SemaphoreType.DMA((11 + kv_half // ATT_DIM * 2 + items + 3 * group_pieces // 2,)),
-        pltpu.SemaphoreType.DMA((4,)),
+        pltpu.SemaphoreType.DMA((7,)),
     ]
     raw, sums, attended = pl.pallas_call(
         functools.partial(pair_kernel, lax.axis_size("ctx")),
@@ -926,7 +952,7 @@
             pltpu.VMEM((8 * GROUPS, tok), F32),
             pltpu.VMEM((part, 4 * q_half), BF16),
         ),
-        in_specs=[pl.BlockSpec(memory_space=pltpu.SMEM)] + [any_spec] * 8 + [vmem_spec] * 2,
+        in_specs=[any_spec] * 11,
         out_specs=(vmem_spec, vmem_spec, vmem_spec),
         scratch_shapes=scratch,
         compiler_params=pltpu.CompilerParams(collective_id=0, has_side_effects=True),

time: 39.9 us -> 38.9 us (0.975)
  Pallas kernels: 38.6 us -> 38.1 us
    pallas_call x1, Pallas kernels: 37.2 us -> 36.7 us  [local_pair(): pl.pallas_call(functools.partial(pair_kernel, lax.axis_size('ctx')), out_...]
where the time goes in v4:
time: 38.9 us; the launch traced here: 38.7 us
  Pallas kernels  38.1 us (98%)
  between operations  0.64 us (2%)
    pallas_call x1, Pallas kernels, local_pair(): pl.pallas_call(functools.partial(pair_kernel, lax.axis_size('ctx')), out_...  36.7 us
    pallas_call x1, Pallas kernels, local_pair(): pl.pallas_call(scale_kernel, out_shape=(jax.ShapeDtypeStruct((part, 4 * h...  1.41 us

profile of v4, /device:TPU:25, one launch (start us, length us, event | category | flops | bytes accessed | tf_op | source)
XLA Modules:
  0.0 38.7 jit_solution(5890285446941433114)
XLA Ops:
  0.6 36.7 %shard_map.122 = (bf16[64,64,128]{2,1,0:T(8,128)(2,1)S(1)}, f32[64,128]{1,0:T(8,128)S(1)}, bf16[64,8192]{1,0:T(8,128)(2,1)S(1)}) custom-call(s32[32]{0:T(128)} %lengths_in.1, bf16[128,4096]{1,0:T(8,128)(2,1)} %x_in.1, bf16[128,4096]{1,0:T(8,128)(2,1)} %gate_in.1, bf16[128,1024]{1,0:T(8,128)(2,1)} %b_in.1, bf16[128,1024]{1,0:T(8,128)(2,1)} %c_in.1, ...), custom_call_target="tpu_custom_call" | custom-call | tf_op jit(solution)/shard_map/pallas_call | solution.py:948
  37.3 1.4 %shard_map.123 = (bf16[64,8192]{1,0:T(8,128)(2,1)}, bf16[64,8192]{1,0:T(8,128)(2,1)}) custom-call(bf16[64,64,128]{2,1,0:T(8,128)(2,1)S(1)} %get-tuple-element.5.raw, f32[64,128]{1,0:T(8,128)S(1)} %get-tuple-element.6.sums, bf16[64,8192]{1,0:T(8,128)(2,1)S(1)} %get-tuple-element.7.attended), custom_call_target="tpu_custom_call" | custom-call | tf_op jit(solution)/shard_map/pallas_call | solution.py:972

commit v5 on v4

--- a/solution.py
+++ b/solution.py
@@ -198,7 +198,7 @@
 ROWS_FIRST = (((0,), (0,)), ((), ()))
 PIECE = 128
 HEADS_AT_ONCE = 2
-MERGE_AFTER = (3, 5)
+MERGE_AFTER = (2, 4)
 PASS_AFTER = (7,)
 
 
@@ -383,19 +383,21 @@
     near_recv = [slots(1) for head in range(kv_heads)]
     far_recv = [slots(1) for head in range(kv_heads)]
     early = base + 8 < n
+    loose = early & ((base + 12 < n) | (base < 4))
     items = []
     for head in range(1, kv_heads):
-        items += [(0, head, early), (1, head, early & ((base + 12 < n) | (base < 4)))]
+        items += [(0, head, 0, ahead), (0, head, 1, early)]
+        items += [(1, head, 0, loose), (1, head, 1, loose)]
     item_send, loan_recv = slots(0, len(items)), slots(1, len(items))
 
     def head_cols(head):
         return slice(head * ATT_DIM, (head + 1) * ATT_DIM)
 
-    def send_part(k, head, dst, step, skip, send, recv):
+    def send_part(k, head, dst, step, at, send, recv):
         for core in range(2):
             remote(
                 part_of((k_in, v_in)[k], core, head * ATT_DIM, ATT_DIM, kv_width),
-                dst.at[pl.ds(at_mine + skip, tok), :],
+                dst.at[pl.ds(at, tok), :],
                 (base + step + core, tp),
                 send,
                 recv,
@@ -407,45 +409,44 @@
             for head in range(kv_heads):
                 for k in range(2):
                     near = kv_s.at[k, :, head_cols(head)]
-                    send_part(k, head, near, 2, rows, near_send, near_recv[head])
+                    send_part(k, head, near, 2, at_mine + rows, near_send, near_recv[head])
 
         @pl.when((odd == 1) & ahead)
         def _():
             for k in range(2):
                 near = kv_s.at[k, :, head_cols(0)]
-                send_part(k, 0, near, 2, rows, near_send, near_recv[0])
-
-        for j, (k, head, lent) in enumerate(items):
-
-            @pl.when((odd == 1) & lent)
+                send_part(k, 0, near, 2, at_mine + rows, near_send, near_recv[0])
+
+    def send_items(lending):
+        for j, (k, head, core, lent) in enumerate(items):
+            there = lent if lending else ahead & jnp.logical_not(lent)
+
+            @pl.when((odd == 1) & (parity == core) & there)
             def _():
-                send_part(k, head, loan_s.at[j], -2, 0, item_send + j, loan_recv + j)
-
-    def send_rest():
-        for j, (k, head, lent) in enumerate(items):
-
-            @pl.when((odd == 1) & ahead & jnp.logical_not(lent))
-            def _():
-                near = kv_s.at[k, :, head_cols(head)]
-                send_part(k, head, near, 2, rows, item_send + j, near_recv[head])
+                if lending:
+                    send_part(k, head, loan_s.at[j], -2, 0, item_send + j, loan_recv + j)
+                else:
+                    near = kv_s.at[k, :, head_cols(head)]
+                    send_part(k, head, near, 2, at_mine + rows, item_send + j, near_recv[head])
 
     def send_far(head):
         @pl.when(ahead)
         def _():
             for k in range(2):
                 far = kv_s.at[k, :, head_cols(head)]
-                send_part(k, head, far, 4, 0, far_send, far_recv[head])
+                send_part(k, head, far, 4, at_mine, far_send, far_recv[head])
 
     def arrived(place, recv):
         remote(place, place, core_peer, far_send, recv).wait_recv()
 
     def forward():
-        for j, (k, head, lent) in enumerate(items):
+        for j, (k, head, core, lent) in enumerate(items):
 
             @pl.when((odd == 0) & lent)
             def _():
                 arrived(loan_s.at[j], loan_recv + j)
-                near = kv_s.at[k, rows : 2 * rows, head_cols(head)]
+                at = rows + core * tok
+                near = kv_s.at[k, at : at + tok, head_cols(head)]
                 peer = (index + 4, tp)
                 remote(loan_s.at[j], near, peer, item_send + j, near_recv[head]).start()
 
@@ -504,6 +505,7 @@
 
     pl.semaphore_wait(barrier, greeted)
     send_near()
+    send_items(True)
     start_step()
     start_b()
     send_far(0)
@@ -600,7 +602,7 @@
                 for k in range(pairs):
                     first_trip(k).start()
 
-    send_rest()
+    send_items(False)
     for head in range(1, kv_heads):
         send_far(head)
     ready_c()
@@ -694,38 +696,37 @@
     scale = LOG2E * ATT_DIM ** (-0.5)
     kvq = y_s.at[: (2 * kv_width + q_all) * tok * 2 // (width * 4)]
     arrived(kvq, ready_kvq)
+    def attend_heads(kv_cols, step_no, lead, first, count):
+        for r in range(0, rows, tok):
+            seen = slice(r, r + 2 * rows + tok)
+            asked = []
+            for h in range(first, first + count):
+                asked.append(q_s[r : r + tok, lead + h * ATT_DIM : lead + (h + 1) * ATT_DIM])
+            scores = dot(jnp.concatenate(asked, axis=0), kv_s[0, seen, kv_cols], COLS_LAST)
+            scores = scores + jnp.concatenate([bias_s[r : r + tok, seen]] * count, axis=0)
+            top = jnp.max(scores, axis=1, keepdims=True)
+            probs = jnp.exp2((scores - top) * scale)
+            total = jnp.sum(probs, axis=1, keepdims=True)
+            summed = dot(probs.astype(BF16), kv_s[1, seen, kv_cols]) / total
+            for h in range(count):
+                part = summed[h * tok : (h + 1) * tok].astype(BF16)
+                for side in range(2):
+                    owned = part[side * part_rows : (side + 1) * part_rows]
+                    cols = slice((first + h) * ATT_DIM, (first + h + 1) * ATT_DIM)
+                    attended_s[step_no, r // tok * 2 + side, :, cols] = owned
+        size = count * ATT_DIM
+        at = pl.multiple_of((tp * 2 + parity) * q_all + lead + first * ATT_DIM, 128)
+        home = attended_out.at[:, pl.ds(at, size)]
+        cols = slice(first * ATT_DIM, first * ATT_DIM + size)
+        here = attended_s.at[step_no]
+        leave(lambda core, side: here.at[core * 2 + side, :, cols], home)
+
     def attend(kv_head):
         step_no = kv_head * q_width // (HEADS_AT_ONCE * ATT_DIM)
         kv_cols = slice(kv_head * ATT_DIM, (kv_head + 1) * ATT_DIM)
         wait_past(kv_head)
         for lead in range(kv_head * q_width, (kv_head + 1) * q_width, HEADS_AT_ONCE * ATT_DIM):
-            for r in range(0, rows, tok):
-                seen = slice(r, r + 2 * rows + tok)
-                asked = jnp.concatenate(
-                    [
-                        q_s[r : r + tok, lead + h * ATT_DIM : lead + (h + 1) * ATT_DIM]
-                        for h in range(HEADS_AT_ONCE)
-                    ],
-                    axis=0,
-                )
-                scores = dot(asked, kv_s[0, seen, kv_cols], COLS_LAST)
-                bias = bias_s[r : r + tok, seen]
-                scores = scores + jnp.concatenate([bias] * HEADS_AT_ONCE, axis=0)
-                top = jnp.max(scores, axis=1, keepdims=True)
-                probs = jnp.exp2((scores - top) * scale)
-                total = jnp.sum(probs, axis=1, keepdims=True)
-                summed = dot(probs.astype(BF16), kv_s[1, seen, kv_cols]) / total
-                for h in range(HEADS_AT_ONCE):
-                    part = summed[h * tok : (h + 1) * tok].astype(BF16)
-                    for side in range(2):
-                        owned = part[side * part_rows : (side + 1) * part_rows]
-                        cols = slice(h * ATT_DIM, (h + 1) * ATT_DIM)
-                        attended_s[step_no, r // tok * 2 + side, :, cols] = owned
-            size = HEADS_AT_ONCE * ATT_DIM
-            at = pl.multiple_of((tp * 2 + parity) * q_all + lead, 128)
-            home = attended_out.at[:, pl.ds(at, size)]
-            here = attended_s.at[step_no]
-            leave(lambda core, side: here.at[core * 2 + side], home)
+            attend_heads(kv_cols, step_no, lead, 0, HEADS_AT_ONCE)
             if step_no == 0:
                 forward()
             for k in range(len(MERGE_AFTER)):
@@ -826,11 +827,12 @@
     def _():
         remote(sent, sent, core_peer, far_send, loan_recv).wait_send()
 
-    for j, (k, head, lent) in enumerate(items):
-
-        @pl.when(lent | ((odd == 1) & ahead))
-        def _():
-            remote(loan_s.at[j], loan_s.at[j], core_peer, item_send + j, loan_recv).wait_send()
+    for j, (k, head, core, lent) in enumerate(items):
+        part = kv_s.at[0, :rows, head_cols(0)]
+        closing = remote(part, part, core_peer, item_send + j, loan_recv)
+        pl.when((odd == 1) & ahead & (parity == core))(closing.wait_send)
+        closing = remote(loan_s.at[j], loan_s.at[j], core_peer, item_send + j, loan_recv)
+        pl.when((odd == 0) & lent)(closing.wait_send)
 
     @pl.when(odd == 0)
     def _():
@@ -907,7 +909,7 @@
     vmem_spec = pl.BlockSpec(memory_space=pltpu.VMEM)
     part = rows // 4
     group_pieces = pieces // groups
-    items = 2 * kv_half // ATT_DIM - 2
+    items = 4 * (kv_half // ATT_DIM - 1)
     step_width = HEADS_AT_ONCE * ATT_DIM
     state_piece = pltpu.VMEM((group_pieces, state, PIECE), BF16)
     scratch = [
@@ -927,7 +929,7 @@
         pltpu.VMEM((8, 128), F32),
         pltpu.VMEM((8, 128), F32),
         pltpu.VMEM((8, half // groups), F32),
-        pltpu.VMEM((items, rows, ATT_DIM), BF16),
+        pltpu.VMEM((items, tok, ATT_DIM), BF16),
         pltpu.SMEM(doc_lengths.shape, jnp.int32),
         pltpu.VMEM((1, decay_rate.shape[0]), F32),
         pltpu.VMEM((1, norm_weight.shape[0]), F32),

time: 38.9 us -> 38.7 us (level)
  Pallas kernels: 38.1 us -> 37.4 us
    pallas_call x1, Pallas kernels: 36.7 us -> 36 us  [local_pair(): pl.pallas_call(functools.partial(pair_kernel, lax.axis_size('ctx')), out_...]
where the time goes in v5:
time: 38.7 us; the launch traced here: 38.2 us
  Pallas kernels  37.4 us (97%)
  between operations  0.8 us (2%)
    pallas_call x1, Pallas kernels, local_pair(): pl.pallas_call(functools.partial(pair_kernel, lax.axis_size('ctx')), out_...  36 us
    pallas_call x1, Pallas kernels, local_pair(): pl.pallas_call(scale_kernel, out_shape=(jax.ShapeDtypeStruct((part, 4 * h...  1.41 us

profile of v5, /device:TPU:25, one launch (start us, length us, event | category | flops | bytes accessed | tf_op | source)
XLA Modules:
  0.0 38.2 jit_solution(15854995983577991951)
XLA Ops:
  0.6 36.0 %shard_map.122 = (bf16[64,64,128]{2,1,0:T(8,128)(2,1)S(1)}, f32[64,128]{1,0:T(8,128)S(1)}, bf16[64,8192]{1,0:T(8,128)(2,1)S(1)}) custom-call(s32[32]{0:T(128)} %lengths_in.1, bf16[128,4096]{1,0:T(8,128)(2,1)} %x_in.1, bf16[128,4096]{1,0:T(8,128)(2,1)} %gate_in.1, bf16[128,1024]{1,0:T(8,128)(2,1)} %b_in.1, bf16[128,1024]{1,0:T(8,128)(2,1)} %c_in.1, ...), custom_call_target="tpu_custom_call" | custom-call | tf_op jit(solution)/shard_map/pallas_call | solution.py:950
  36.6 1.4 %shard_map.123 = (bf16[64,8192]{1,0:T(8,128)(2,1)}, bf16[64,8192]{1,0:T(8,128)(2,1)}) custom-call(bf16[64,64,128]{2,1,0:T(8,128)(2,1)S(1)} %get-tuple-element.5.raw, f32[64,128]{1,0:T(8,128)S(1)} %get-tuple-element.6.sums, bf16[64,8192]{1,0:T(8,128)(2,1)S(1)} %get-tuple-element.7.attended), custom_call_target="tpu_custom_call" | custom-call | tf_op jit(solution)/shard_map/pallas_call | solution.py:974

commit v6 on v5

--- a/solution.py
+++ b/solution.py
@@ -200,6 +200,16 @@
 HEADS_AT_ONCE = 2
 MERGE_AFTER = (2, 4)
 PASS_AFTER = (7,)
+FIRST_HEAD_ORDER = (
+    (0, 0, 1),
+    (1, 0, 1),
+    (0, 0, 0),
+    (0, 1, 1),
+    (1, 1, 1),
+    (1, 0, 0),
+    (0, 1, 0),
+    (1, 1, 0),
+)
 
 
 def dot(a, b, dims=(((1,), (0,)), ((), ())), precision=None):
@@ -393,8 +403,8 @@
     def head_cols(head):
         return slice(head * ATT_DIM, (head + 1) * ATT_DIM)
 
-    def send_part(k, head, dst, step, at, send, recv):
-        for core in range(2):
+    def send_part(k, head, dst, step, at, send, recv, cores=(0, 1)):
+        for core in cores:
             remote(
                 part_of((k_in, v_in)[k], core, head * ATT_DIM, ATT_DIM, kv_width),
                 dst.at[pl.ds(at, tok), :],
@@ -413,9 +423,12 @@
 
         @pl.when((odd == 1) & ahead)
         def _():
-            for k in range(2):
-                near = kv_s.at[k, :, head_cols(0)]
-                send_part(k, 0, near, 2, at_mine + rows, near_send, near_recv[0])
+            for k, far, core in FIRST_HEAD_ORDER:
+                place = kv_s.at[k, :, head_cols(0)]
+                if far:
+                    send_part(k, 0, place, 4, at_mine, far_send, far_recv[0], (core,))
+                else:
+                    send_part(k, 0, place, 2, at_mine + rows, near_send, near_recv[0], (core,))
 
     def send_items(lending):
         for j, (k, head, core, lent) in enumerate(items):
@@ -430,7 +443,7 @@
                     send_part(k, head, near, 2, at_mine + rows, item_send + j, near_recv[head])
 
     def send_far(head):
-        @pl.when(ahead)
+        @pl.when(ahead & ((odd == 0) | (head > 0)))
         def _():
             for k in range(2):
                 far = kv_s.at[k, :, head_cols(head)]
@@ -721,6 +734,10 @@
         here = attended_s.at[step_no]
         leave(lambda core, side: here.at[core * 2 + side, :, cols], home)
 
+    def merge_first():
+        coefficients()
+        merge(0)
+
     def attend(kv_head):
         step_no = kv_head * q_width // (HEADS_AT_ONCE * ATT_DIM)
         kv_cols = slice(kv_head * ATT_DIM, (kv_head + 1) * ATT_DIM)
@@ -732,8 +749,9 @@
             for k in range(len(MERGE_AFTER)):
                 if MERGE_AFTER[k] == step_no:
                     if k == 0:
-                        coefficients()
-                    merge(k)
+                        pl.when(pair > 0)(merge_first)
+                    else:
+                        merge(k)
             for k in range(len(PASS_AFTER)):
                 if PASS_AFTER[k] == step_no:
                     pass_on(k)
@@ -745,6 +763,7 @@
         pl.when(attend_now)(functools.partial(attend, 0))
         pl.when(jnp.logical_not(attend_now))(intra)
 
+    pl.when(pair == 0)(merge_first)
     for kv_head in range(1, kv_heads):
         attend(kv_head)
 

time: 38.7 us -> 38.5 us (level)
  no operation moved by 1% of the time
where the time goes in v6:
time: 38.5 us; the launch traced here: 38.2 us
  Pallas kernels  37.4 us (97%)
  between operations  0.8 us (2%)
    pallas_call x1, Pallas kernels, local_pair(): pl.pallas_call(functools.partial(pair_kernel, lax.axis_size('ctx')), out_...  36 us
    pallas_call x1, Pallas kernels, local_pair(): pl.pallas_call(scale_kernel, out_shape=(jax.ShapeDtypeStruct((part, 4 * h...  1.41 us

profile of v6, /device:TPU:25, one launch (start us, length us, event | category | flops | bytes accessed | tf_op | source)
XLA Modules:
  0.0 38.2 jit_solution(16975662401531555505)
XLA Ops:
  0.6 36.0 %shard_map.122 = (bf16[64,64,128]{2,1,0:T(8,128)(2,1)S(1)}, f32[64,128]{1,0:T(8,128)S(1)}, bf16[64,8192]{1,0:T(8,128)(2,1)S(1)}) custom-call(s32[32]{0:T(128)} %lengths_in.1, bf16[128,4096]{1,0:T(8,128)(2,1)} %x_in.1, bf16[128,4096]{1,0:T(8,128)(2,1)} %gate_in.1, bf16[128,1024]{1,0:T(8,128)(2,1)} %b_in.1, bf16[128,1024]{1,0:T(8,128)(2,1)} %c_in.1, ...), custom_call_target="tpu_custom_call" | custom-call | tf_op jit(solution)/shard_map/pallas_call | solution.py:969
  36.6 1.4 %shard_map.123 = (bf16[64,8192]{1,0:T(8,128)(2,1)}, bf16[64,8192]{1,0:T(8,128)(2,1)}) custom-call(bf16[64,64,128]{2,1,0:T(8,128)(2,1)S(1)} %get-tuple-element.5.raw, f32[64,128]{1,0:T(8,128)S(1)} %get-tuple-element.6.sums, bf16[64,8192]{1,0:T(8,128)(2,1)S(1)} %get-tuple-element.7.attended), custom_call_target="tpu_custom_call" | custom-call | tf_op jit(solution)/shard_map/pallas_call | solution.py:993

commit v7 on v6

--- a/solution.py
+++ b/solution.py
@@ -643,15 +643,15 @@
                     y_s[r : r + tok, lead : lead + 128] = whole
 
     part_rows = rows // 4
-    exits = ((tp_peer, 0, 1), (cross_peer, 1, 1), (core_peer, 1, 0))
 
     exit_send, exit_recv, exit_own = slots(0), slots(1), slots(2)
     sums_send, sums_recv, sums_own = slots(0), slots(1), slots(2)
 
     def leave(piece_for, home, send=exit_send, recv=exit_recv, own=exit_own):
-        for peer, far_core, far_tp in exits:
-            src = piece_for(other if far_core else parity, 1 - tp if far_tp else tp)
-            remote(src, home, peer, send, recv).start()
+        for core in (1, 0):
+            peer = (base + core, 1 - tp)
+            remote(piece_for(core, 1 - tp), home, peer, send, recv).start()
+        remote(piece_for(other, tp), home, core_peer, send, recv).start()
         pltpu.make_async_copy(piece_for(parity, tp), home, own_sem.at[own]).start()
 
     def settle(thrice, once, send, recv, own):
@@ -709,30 +709,34 @@
     scale = LOG2E * ATT_DIM ** (-0.5)
     kvq = y_s.at[: (2 * kv_width + q_all) * tok * 2 // (width * 4)]
     arrived(kvq, ready_kvq)
-    def attend_heads(kv_cols, step_no, lead, first, count):
-        for r in range(0, rows, tok):
+    def attend_heads(kv_cols, step_no, lead):
+        at = pl.multiple_of((tp * 2 + parity) * q_all + lead, 128)
+        home = attended_out.at[:, pl.ds(at, HEADS_AT_ONCE * ATT_DIM)]
+        here = attended_s.at[step_no]
+        for core in range(2):
+            r = core * tok
             seen = slice(r, r + 2 * rows + tok)
             asked = []
-            for h in range(first, first + count):
+            for h in range(HEADS_AT_ONCE):
                 asked.append(q_s[r : r + tok, lead + h * ATT_DIM : lead + (h + 1) * ATT_DIM])
             scores = dot(jnp.concatenate(asked, axis=0), kv_s[0, seen, kv_cols], COLS_LAST)
-            scores = scores + jnp.concatenate([bias_s[r : r + tok, seen]] * count, axis=0)
+            scores = scores + jnp.concatenate([bias_s[r : r + tok, seen]] * HEADS_AT_ONCE, axis=0)
             top = jnp.max(scores, axis=1, keepdims=True)
             probs = jnp.exp2((scores - top) * scale)
             total = jnp.sum(probs, axis=1, keepdims=True)
             summed = dot(probs.astype(BF16), kv_s[1, seen, kv_cols]) / total
-            for h in range(count):
+            for h in range(HEADS_AT_ONCE):
                 part = summed[h * tok : (h + 1) * tok].astype(BF16)
                 for side in range(2):
                     owned = part[side * part_rows : (side + 1) * part_rows]
-                    cols = slice((first + h) * ATT_DIM, (first + h + 1) * ATT_DIM)
-                    attended_s[step_no, r // tok * 2 + side, :, cols] = owned
-        size = count * ATT_DIM
-        at = pl.multiple_of((tp * 2 + parity) * q_all + lead + first * ATT_DIM, 128)
-        home = attended_out.at[:, pl.ds(at, size)]
-        cols = slice(first * ATT_DIM, first * ATT_DIM + size)
-        here = attended_s.at[step_no]
-        leave(lambda core, side: here.at[core * 2 + side, :, cols], home)
+                    cols = slice(h * ATT_DIM, (h + 1) * ATT_DIM)
+                    attended_s[step_no, core * 2 + side, :, cols] = owned
+            if step_no == 0 or core == 1:
+                for half in (core,) if step_no == 0 else (1, 0):
+                    src, peer = here.at[half * 2 + 1 - tp], (base + half, 1 - tp)
+                    remote(src, home, peer, exit_send, exit_recv).start()
+        remote(here.at[other * 2 + tp], home, core_peer, exit_send, exit_recv).start()
+        pltpu.make_async_copy(here.at[parity * 2 + tp], home, own_sem.at[exit_own]).start()
 
     def merge_first():
         coefficients()
@@ -743,7 +747,7 @@
         kv_cols = slice(kv_head * ATT_DIM, (kv_head + 1) * ATT_DIM)
         wait_past(kv_head)
         for lead in range(kv_head * q_width, (kv_head + 1) * q_width, HEADS_AT_ONCE * ATT_DIM):
-            attend_heads(kv_cols, step_no, lead, 0, HEADS_AT_ONCE)
+            attend_heads(kv_cols, step_no, lead)
             if step_no == 0:
                 forward()
             for k in range(len(MERGE_AFTER)):

time: 38.5 us -> 38.4 us (level)
  no operation moved by 1% of the time
where the time goes in v7:
time: 38.4 us; the launch traced here: 38.2 us
  Pallas kernels  37.4 us (97%)
  between operations  0.8 us (2%)
    pallas_call x1, Pallas kernels, local_pair(): pl.pallas_call(functools.partial(pair_kernel, lax.axis_size('ctx')), out_...  36 us
    pallas_call x1, Pallas kernels, local_pair(): pl.pallas_call(scale_kernel, out_shape=(jax.ShapeDtypeStruct((part, 4 * h...  1.41 us

profile of v7, /device:TPU:25, one launch (start us, length us, event | category | flops | bytes accessed | tf_op | source)
XLA Modules:
  0.0 38.2 jit_solution(10461651690986139348)
XLA Ops:
  0.6 36.0 %shard_map.122 = (bf16[64,64,128]{2,1,0:T(8,128)(2,1)S(1)}, f32[64,128]{1,0:T(8,128)S(1)}, bf16[64,8192]{1,0:T(8,128)(2,1)S(1)}) custom-call(s32[32]{0:T(128)} %lengths_in.1, bf16[128,4096]{1,0:T(8,128)(2,1)} %x_in.1, bf16[128,4096]{1,0:T(8,128)(2,1)} %gate_in.1, bf16[128,1024]{1,0:T(8,128)(2,1)} %b_in.1, bf16[128,1024]{1,0:T(8,128)(2,1)} %c_in.1, ...), custom_call_target="tpu_custom_call" | custom-call | tf_op jit(solution)/shard_map/pallas_call | solution.py:973
  36.6 1.4 %shard_map.123 = (bf16[64,8192]{1,0:T(8,128)(2,1)}, bf16[64,8192]{1,0:T(8,128)(2,1)}) custom-call(bf16[64,64,128]{2,1,0:T(8,128)(2,1)S(1)} %get-tuple-element.5.raw, f32[64,128]{1,0:T(8,128)S(1)} %get-tuple-element.6.sums, bf16[64,8192]{1,0:T(8,128)(2,1)S(1)} %get-tuple-element.7.attended), custom_call_target="tpu_custom_call" | custom-call | tf_op jit(solution)/shard_map/pallas_call | solution.py:997

commit v8 on v7

--- a/solution.py
+++ b/solution.py
@@ -198,7 +198,7 @@
 ROWS_FIRST = (((0,), (0,)), ((), ()))
 PIECE = 128
 HEADS_AT_ONCE = 2
-MERGE_AFTER = (2, 4)
+MERGE_AFTER = (3, 4)
 PASS_AFTER = (7,)
 FIRST_HEAD_ORDER = (
     (0, 0, 1),

time: 38.4 us -> 38.4 us (level)
  no operation moved by 1% of the time
where the time goes in v8:
time: 38.4 us; the launch traced here: 38.2 us
  Pallas kernels  37.4 us (97%)
  between operations  0.8 us (2%)
    pallas_call x1, Pallas kernels, local_pair(): pl.pallas_call(functools.partial(pair_kernel, lax.axis_size('ctx')), out_...  36 us
    pallas_call x1, Pallas kernels, local_pair(): pl.pallas_call(scale_kernel, out_shape=(jax.ShapeDtypeStruct((part, 4 * h...  1.41 us

profile of v8, /device:TPU:25, one launch (start us, length us, event | category | flops | bytes accessed | tf_op | source)
XLA Modules:
  0.0 38.2 jit_solution(1133428492112015556)
XLA Ops:
  0.6 36.0 %shard_map.122 = (bf16[64,64,128]{2,1,0:T(8,128)(2,1)S(1)}, f32[64,128]{1,0:T(8,128)S(1)}, bf16[64,8192]{1,0:T(8,128)(2,1)S(1)}) custom-call(s32[32]{0:T(128)} %lengths_in.1, bf16[128,4096]{1,0:T(8,128)(2,1)} %x_in.1, bf16[128,4096]{1,0:T(8,128)(2,1)} %gate_in.1, bf16[128,1024]{1,0:T(8,128)(2,1)} %b_in.1, bf16[128,1024]{1,0:T(8,128)(2,1)} %c_in.1, ...), custom_call_target="tpu_custom_call" | custom-call | tf_op jit(solution)/shard_map/pallas_call | solution.py:973
  36.6 1.4 %shard_map.123 = (bf16[64,8192]{1,0:T(8,128)(2,1)}, bf16[64,8192]{1,0:T(8,128)(2,1)}) custom-call(bf16[64,64,128]{2,1,0:T(8,128)(2,1)S(1)} %get-tuple-element.5.raw, f32[64,128]{1,0:T(8,128)S(1)} %get-tuple-element.6.sums, bf16[64,8192]{1,0:T(8,128)(2,1)S(1)} %get-tuple-element.7.attended), custom_call_target="tpu_custom_call" | custom-call | tf_op jit(solution)/shard_map/pallas_call | solution.py:997
